TPU v7x, 256 devices: a whole 4x4x8 slice. The times are simulated.
256 devices in a mesh: leaf: 64 (over z, x, core), sub: 4 (over y).
Axes of the slice: x: 4, y: 4, z: 8, core: 2. Of those that a mesh axis runs over, the one named last changes fastest.
Arguments:
- points: bfloat16 [1048576, 64], P(('leaf', 'sub')), may hold values from -6 to 6
- probes: bfloat16 [1048576, 128], P(('leaf', 'sub')), may hold values from -6 to 6
- order: int32 [1048576], P(('leaf', 'sub')), may hold values from 0 to 511, as said below
- near_lists: int32 [2048, 12], P(('leaf', 'sub')), may hold values from 0 to 2047, as said below
- near_counts: int32 [2048], P(('leaf', 'sub')), may hold values from 1 to 12, as said below
- leaf_sets: int32 [2048, 128], P(('leaf', 'sub')), may hold values from 0 to 511, as said below
- merge_sets: int32 [2047, 128], replicated, may hold values from 0 to 255, as said below
Outputs:
- near_samples: float32 [1048576, 128], P(('leaf', 'sub'))
- root_samples: float32 [16384], P(('leaf', 'sub'))
Inputs may be any that keep to these rules, and one draw needn't show every extreme that they name: `order`: the 512 entries of each leaf block are a permutation of 0 to 511. `near_lists`: for block g of shard i = g // 32: entry 0 is g; entries 1 to near_counts[g] - 1 are distinct blocks other than g within i * 32 - 8 to (i + 1) * 32 + 7; entries from near_counts[g] on equal g. `near_counts`: some block among the first sixteen of the aligned sixteens of blocks has 12 entries. `leaf_sets`: each row holds distinct values. `merge_sets`: each row holds distinct values; row m - 1 belongs to the node whose two children meet at block m.
All inputs are finite; a program needn't handle non-finite values.
Results may differ from a plain program's by a relative error of at most 0.0029.
Values may be sent and summed in bfloat16 or wider, within the bound.
A program may use at most 128 MiB of HBM per device.

v0:
```python
import jax
import jax.numpy as jnp
from jax import lax
from jax.sharding import PartitionSpec as P


def padded(shard, sides, width):
    for axis, dim in sides:
        size, length = (lax.axis_size(axis), shard.shape[dim])
        up = [(i, (i + 1) % size) for i in range(size - 1)]
        down = [(j, i) for i, j in up]
        last = lax.slice_in_dim(shard, length - width, length, axis=dim)
        initial = lax.slice_in_dim(shard, 0, width, axis=dim)
        before = lax.ppermute(last, axis, up)
        after = lax.ppermute(initial, axis, down)
        shard = jnp.concatenate([before, shard, after], axis=dim)
    return shard


def partner(shard, axis, distance):
    return lax.ppermute(shard, axis, [(i, i ^ 1 << distance) for i in range(lax.axis_size(axis))])


def row_squares(values):
    return jnp.sum(jnp.square(values.astype(jnp.float32)), axis=-1)


def kernel_tile(target_rows, target_sq, source_rows, source_sq):
    cross_terms = jnp.dot(target_rows, source_rows.T, preferred_element_type=jnp.float32)
    distance = target_sq[:, None] + source_sq[None, :] - 2.0 * cross_terms
    return jnp.exp(-distance / target_rows.shape[1])


def apply_tiles(weights, source_rows):
    return jnp.dot(weights, source_rows, preferred_element_type=jnp.float32)


def condense(coords, samples, chosen):
    picked = jnp.take(coords, chosen, axis=0)
    weights = kernel_tile(picked, row_squares(picked), coords, row_squares(coords))
    totals = jnp.sum(weights, axis=1, keepdims=True)
    mixed_part = jnp.dot(
        weights, samples, precision=lax.Precision.HIGHEST, preferred_element_type=jnp.float32
    )
    return (picked, jnp.take(samples, chosen, axis=0) + mixed_part / totals)


def merge_levels(coords, samples, merge_sets, first_block, node_span):
    while coords.shape[0] > 1:
        node_count = coords.shape[0] // 2
        node_first = first_block + jnp.arange(node_count, dtype=jnp.int32) * (2 * node_span)
        chosen = jnp.take(merge_sets, node_first + node_span - 1, axis=0)
        coords, samples = jax.vmap(condense)(
            coords.reshape(node_count, 2 * coords.shape[1], coords.shape[2]),
            samples.reshape(node_count, 2 * samples.shape[1], samples.shape[2]),
            chosen,
        )
        node_span = node_span * 2
    return (coords[0], samples[0], node_span)


def pair_step(coords, samples, other_coords, other_samples, merge_sets, first_block, node_span):
    right_side = first_block // node_span % 2 == 1
    node_first = first_block // (2 * node_span) * (2 * node_span)
    chosen = lax.dynamic_index_in_dim(merge_sets, node_first + node_span - 1, 0, keepdims=False)
    other_coords = other_coords.astype(jnp.bfloat16)
    left_coords = jnp.where(right_side, other_coords, coords)
    right_coords = jnp.where(right_side, coords, other_coords)
    left_samples = jnp.where(right_side, other_samples, samples)
    right_samples = jnp.where(right_side, samples, other_samples)
    coords, samples = condense(
        jnp.concatenate([left_coords, right_coords], axis=0),
        jnp.concatenate([left_samples, right_samples], axis=0),
        chosen,
    )
    return (coords, samples, node_span * 2)


def on_device(points, probes, order, near_lists, near_counts, leaf_sets, merge_sets):
    sub_count = lax.axis_size("sub")
    leaf_count = lax.axis_size("leaf")
    blocks_dev = leaf_sets.shape[0]
    leaf_rows = points.shape[0] // blocks_dev
    feature_dim = points.shape[1]
    probe_cols = probes.shape[1]
    shard_count = sub_count * blocks_dev
    leaf_index = lax.axis_index("leaf")
    sub_index = lax.axis_index("sub")
    device_rank = leaf_index * sub_count + sub_index
    first_block = device_rank * blocks_dev
    local_base = jnp.arange(points.shape[0], dtype=jnp.int32) // leaf_rows * leaf_rows
    tree_points = jnp.take(points, order + local_base, axis=0)
    window_start = leaf_index * shard_count - blocks_dev
    last_slot = near_lists.shape[1] - 1
    lane_index = jnp.arange(blocks_dev, dtype=jnp.int32)
    shard_points, shard_probes = (
        lax.all_gather(tree_points, "sub", axis=0, tiled=True),
        lax.all_gather(probes, "sub", axis=0, tiled=True),
    )
    around_points, around_probes = (
        padded(shard_points, (("leaf", 0),), blocks_dev * leaf_rows),
        padded(shard_probes, (("leaf", 0),), blocks_dev * leaf_rows),
    )
    window_blocks = shard_count + 2 * blocks_dev
    around_points = around_points.reshape(window_blocks, leaf_rows, feature_dim)
    around_probes = around_probes.reshape(window_blocks, leaf_rows, probe_cols)
    around_sq = row_squares(around_points)
    tile_batch = jax.vmap(kernel_tile)
    apply_batch = jax.vmap(apply_tiles)
    own_points = tree_points.reshape(blocks_dev, leaf_rows, feature_dim)
    own_sq = row_squares(own_points)
    local_lists = near_lists - window_start
    own_starts = jnp.cumsum(near_counts) - near_counts
    own_total = jnp.sum(near_counts)
    own_turns = (own_total + blocks_dev - 1) // blocks_dev

    def add_own(step_index, running):
        pair_index = step_index * blocks_dev + lane_index
        owner_block = (
            jnp.sum((own_starts[None, :] <= pair_index[:, None]).astype(jnp.int32), axis=1) - 1
        )
        slot_index = jnp.minimum(pair_index - jnp.take(own_starts, owner_block, axis=0), last_slot)
        targets = local_lists[owner_block, slot_index]
        weights = tile_batch(
            jnp.take(own_points, owner_block, axis=0),
            jnp.take(own_sq, owner_block, axis=0),
            jnp.take(around_points, targets, axis=0),
            jnp.take(around_sq, targets, axis=0),
        )
        live_mask = pair_index < own_total
        weights = jnp.where(live_mask[:, None, None], weights, 0.0).astype(jnp.bfloat16)
        return running.at[owner_block].add(
            apply_batch(weights, jnp.take(around_probes, targets, axis=0))
        )

    running = lax.fori_loop(
        0, own_turns, add_own, jnp.zeros((blocks_dev, leaf_rows, probe_cols), jnp.float32)
    )
    near_samples = (running * leaf_rows ** (-0.5)).reshape(blocks_dev * leaf_rows, probe_cols)
    coords, samples = jax.vmap(condense)(
        tree_points.reshape(blocks_dev, leaf_rows, feature_dim),
        probes.reshape(blocks_dev, leaf_rows, probe_cols).astype(jnp.float32),
        leaf_sets,
    )
    coords, samples, node_span = merge_levels(coords, samples, merge_sets, first_block, 1)
    for bit_index in range(sub_count.bit_length() - 1):
        other_coords, other_samples = partner(
            (coords.astype(jnp.float32), samples), "sub", bit_index
        )
        coords, samples, node_span = pair_step(
            coords, samples, other_coords, other_samples, merge_sets, first_block, node_span
        )
    for bit_index in range(leaf_count.bit_length() - 1):
        other_coords, other_samples = partner(
            (coords.astype(jnp.float32), samples), "leaf", bit_index
        )
        coords, samples, node_span = pair_step(
            coords, samples, other_coords, other_samples, merge_sets, first_block, node_span
        )
    flat_root = samples.reshape(samples.shape[0] * samples.shape[1])
    piece_len = flat_root.shape[0] // (sub_count * leaf_count)
    root_piece = lax.dynamic_slice_in_dim(flat_root, device_rank * piece_len, piece_len, 0)
    return (near_samples, root_piece)


def solution(mesh):
    in_specs = (
        P(("leaf", "sub"), None),
        P(("leaf", "sub"), None),
        P(("leaf", "sub")),
        P(("leaf", "sub"), None),
        P(("leaf", "sub")),
        P(("leaf", "sub"), None),
        P(),
    )
    out_specs = (P(("leaf", "sub"), None), P(("leaf", "sub")))
    return jax.shard_map(
        on_device, mesh=mesh, in_specs=in_specs, out_specs=out_specs, check_vma=False
    )
```

profile of v0, /device:TPU:66, one launch (start us, length us, event | category | flops | bytes accessed | tf_op | source)
XLA Modules:
  0.0 418.0 jit_solution(12290781174076603283)
XLA Ops:
  10.2 12.1 %gather_fusion.7 = bf16[4096,64]{1,0:T(8,128)(2,1)S(1)} fusion(bf16[4096,64]{1,0:T(8,128)(2,1)S(1)} %copy.40, s32[4096]{0:T(1024)S(1)} %broadcast_clamp_fusion), kind=kCustom, calls=%fused_computation.23 | custom fusion | bytes 1064960 | tf_op jit(solution)/shard_map/jit(_take)/gather | solution.py:92
  22.4 2.0 multiply_reduce_fusion.1
  30.0 5.8 %gather_fusion.11 = bf16[1024,64]{1,0:T(8,128)(2,1)S(1)} fusion(bf16[8,512,64]{2,1,0:T(8,128)(2,1)S(1)} %broadcast_select_fusion.3, s32[1024]{0:T(1024)S(1)} %fusion.93), kind=kCustom, calls=%fused_computation.27 | custom fusion | bytes 270336 | tf_op jit(solution)/shard_map/vmap(jit(_take))/gather | solution.py:39
  36.1 3.2 gather_fusion.13
  45.0 2.1 collective-permute-start.5
  50.0 11.5 %gather_fusion.10 = f32[1024,128]{1,0:T(8,128)} fusion(f32[8,512,128]{2,1,0:T(8,128)S(1)} %convert_element_type.149, s32[1024]{0:T(1024)S(1)} %fusion.93), kind=kCustom, calls=%fused_computation.26 | custom fusion | bytes 1056768 | tf_op jit(solution)/shard_map/vmap(jit(_take))/gather | solution.py:45
  64.6 3.7 gather_fusion.12
  69.6 1.9 gather_fusion.14
  78.7 3.3 collective-permute-start.7
  82.3 1.9 collective-permute-done.7
  89.1 3.1 collective-permute-done.11
  93.2 2.2 collective-permute-start.13
  96.5 3.3 collective-permute-start.6
  101.4 2.0 collective-permute-start.15
  107.0 4.2 collective-permute-done.17
  112.1 5.5 %collective-permute-start.19 = (bf16[128,64]{1,0:T(8,128)(2,1)S(1)}, bf16[128,64]{1,0:T(8,128)(2,1)S(1)}, u32[]{:S(2)}, u32[]{:S(2)}) collective-permute-start(bf16[128,64]{1,0:T(8,128)(2,1)S(1)} %fusion.123), channel_id=1, source_target_pairs={{0,128},{4,132},{8,136},{12,140},{16,144},{20,148},{24,152},{28,15... | collective-permute-start | bytes 49160 | tf_op jit(solution)/shard_map/ppermute | solution.py:21
  122.8 2.5 collective-permute-done.10
  127.9 4.3 %collective-permute-done.12 = f32[128,128]{1,0:T(8,128)S(1)} collective-permute-done((f32[128,128]{1,0:T(8,128)S(1)}, f32[128,128]{1,0:T(8,128)S(1)}, u32[]{:S(2)}, u32[]{:S(2)}) %collective-permute-start.12) | collective-permute-done | bytes 65568 | tf_op jit(solution)/shard_map/ppermute | solution.py:21
  135.0 2.4 collective-permute-done.14
  140.2 3.6 collective-permute-done.16
  148.1 1.9 collective-permute-start
  150.4 3.6 collective-permute-start.1
  154.1 3.0 fusion.124
  157.1 2.1 collective-permute-start.2
  159.2 3.6 collective-permute-start.3
  166.8 22.0 %multiply_reduce_fusion = (f32[24576]{0:T(1024)S(1)}, bf16[24576,64]{1,0:T(8,128)(2,1)}) fusion(bf16[4096,64]{1,0:T(8,128)(2,1)S(1)} %copy.44, bf16[16384,64]{1,0:T(8,128)(2,1)} %all-gather.3.cloned.1.call-done, bf16[4096,64]{1,0:T(8,128)(2,1)S(1)} %copy.43), kind=kLoop, calls=%fused_computation.74 | loop fusion | flops 14131200 | bytes 6389760 | tf_op jit(solution)/shard_map/reduce_sum | solution.py:25
  188.8 8.5 %pad_maximum_fusion.1 = bf16[24576,128]{1,0:T(8,128)(2,1)} fusion(bf16[4096,128]{1,0:T(8,128)(2,1)} %collective-permute-done.3, bf16[16384,128]{1,0:T(8,128)(2,1)} %all-gather.5.cloned.1.call-done, bf16[4096,128]{1,0:T(8,128)(2,1)} %collective-permute-done.2), kind=kLoop, calls=%fused_computation.76 | loop fusion | flops 18874368 | bytes 12582912 | tf_op jit(solution)/shard_map/concatenate | solution.py:16
  197.5 211.9 %while.16 = (s32[]{:T(128)}, f32[8,512,128]{2,1,0:T(8,128)S(1)}, s32[]{:T(128)}, s32[8]{0:T(128)S(1)}, s32[]{:T(128)}, /*index=5*/f32[8,512]{1,0:T(8,128)S(1)}, ...) while((s32[]{:T(128)}, f32[8,512,128]{2,1,0:T(8,128)S(1)}, ...), condition=%wide.region_7.8_spmd.clone, body=%wide.region_4.7_spmd.clone.sunk | while | flops 821570048 | bytes 14853209 | solution.py:136
  200.5 4.5 %gather_fusion.4 = bf16[8,512,128]{2,1,0:T(8,128)(2,1)} fusion(bf16[48,512,128]{2,1,0:T(8,128)(2,1)} %get-tuple-element.519, s32[1024]{0:T(1024)S(1)} %pad_clamp_fusion.15), kind=kCustom, calls=%fused_computation.6.clone.clone.1 | custom fusion | bytes 2097184 | tf_op jit(solution)/shard_map/while/body/jit(_take)/gather | solution.py:133
  205.0 4.4 %gather_fusion.5 = bf16[8,512,64]{2,1,0:T(8,128)(2,1)} fusion(bf16[48,512,64]{2,1,0:T(8,128)(2,1)} %get-tuple-element.518, s32[1024]{0:T(1024)S(1)} %pad_clamp_fusion.15), kind=kCustom, calls=%fused_computation.5.clone.clone.1 | custom fusion | bytes 1048608 | tf_op jit(solution)/shard_map/while/body/jit(_take)/gather | solution.py:127
  211.7 6.2 %fusion.170 = f32[8,512,128]{2,1,0:T(8,128)} fusion(f32[8,512]{1,0:T(8,128)S(1)} %get-tuple-element.481, f32[8,512]{1,0:T(8,128)S(1)} %get-tuple-element.482, pred[8]{0:T(512)(128)(4,1)S(1)} %broadcast_compare_fusion.2, bf16[8,512,128]{2,1,0:T(8,128)(2,1)} %gather_fusion.4, bf16[8,512,64]{2,1,0:T(8,128)(2,1)} %gather_fusion.5, ...), kind=kOutput, calls=%fused_computation.37.clone.1 | convolution fusion | flops 821035008 | bytes 4227096 | tf_op jit(solution)/shard_map/while/body/vmap()/dot_general | solution.py:35
  217.9 3.3 scatter_fusion
  224.0 4.5 %gather_fusion.4 = bf16[8,512,128]{2,1,0:T(8,128)(2,1)} fusion(bf16[48,512,128]{2,1,0:T(8,128)(2,1)} %get-tuple-element.519, s32[1024]{0:T(1024)S(1)} %pad_clamp_fusion.15), kind=kCustom, calls=%fused_computation.6.clone.clone.1 | custom fusion | bytes 2097184 | tf_op jit(solution)/shard_map/while/body/jit(_take)/gather | solution.py:133
  228.5 4.4 %gather_fusion.5 = bf16[8,512,64]{2,1,0:T(8,128)(2,1)} fusion(bf16[48,512,64]{2,1,0:T(8,128)(2,1)} %get-tuple-element.518, s32[1024]{0:T(1024)S(1)} %pad_clamp_fusion.15), kind=kCustom, calls=%fused_computation.5.clone.clone.1 | custom fusion | bytes 1048608 | tf_op jit(solution)/shard_map/while/body/jit(_take)/gather | solution.py:127
  235.2 6.2 %fusion.170 = f32[8,512,128]{2,1,0:T(8,128)} fusion(f32[8,512]{1,0:T(8,128)S(1)} %get-tuple-element.481, f32[8,512]{1,0:T(8,128)S(1)} %get-tuple-element.482, pred[8]{0:T(512)(128)(4,1)S(1)} %broadcast_compare_fusion.2, bf16[8,512,128]{2,1,0:T(8,128)(2,1)} %gather_fusion.4, bf16[8,512,64]{2,1,0:T(8,128)(2,1)} %gather_fusion.5, ...), kind=kOutput, calls=%fused_computation.37.clone.1 | convolution fusion | flops 821035008 | bytes 4227096 | tf_op jit(solution)/shard_map/while/body/vmap()/dot_general | solution.py:35
  241.4 3.3 scatter_fusion
  247.5 4.5 %gather_fusion.4 = bf16[8,512,128]{2,1,0:T(8,128)(2,1)} fusion(bf16[48,512,128]{2,1,0:T(8,128)(2,1)} %get-tuple-element.519, s32[1024]{0:T(1024)S(1)} %pad_clamp_fusion.15), kind=kCustom, calls=%fused_computation.6.clone.clone.1 | custom fusion | bytes 2097184 | tf_op jit(solution)/shard_map/while/body/jit(_take)/gather | solution.py:133
  252.0 4.4 %gather_fusion.5 = bf16[8,512,64]{2,1,0:T(8,128)(2,1)} fusion(bf16[48,512,64]{2,1,0:T(8,128)(2,1)} %get-tuple-element.518, s32[1024]{0:T(1024)S(1)} %pad_clamp_fusion.15), kind=kCustom, calls=%fused_computation.5.clone.clone.1 | custom fusion | bytes 1048608 | tf_op jit(solution)/shard_map/while/body/jit(_take)/gather | solution.py:127
  258.8 6.2 %fusion.170 = f32[8,512,128]{2,1,0:T(8,128)} fusion(f32[8,512]{1,0:T(8,128)S(1)} %get-tuple-element.481, f32[8,512]{1,0:T(8,128)S(1)} %get-tuple-element.482, pred[8]{0:T(512)(128)(4,1)S(1)} %broadcast_compare_fusion.2, bf16[8,512,128]{2,1,0:T(8,128)(2,1)} %gather_fusion.4, bf16[8,512,64]{2,1,0:T(8,128)(2,1)} %gather_fusion.5, ...), kind=kOutput, calls=%fused_computation.37.clone.1 | convolution fusion | flops 821035008 | bytes 4227096 | tf_op jit(solution)/shard_map/while/body/vmap()/dot_general | solution.py:35
  264.9 3.3 scatter_fusion
  271.0 4.5 %gather_fusion.4 = bf16[8,512,128]{2,1,0:T(8,128)(2,1)} fusion(bf16[48,512,128]{2,1,0:T(8,128)(2,1)} %get-tuple-element.519, s32[1024]{0:T(1024)S(1)} %pad_clamp_fusion.15), kind=kCustom, calls=%fused_computation.6.clone.clone.1 | custom fusion | bytes 2097184 | tf_op jit(solution)/shard_map/while/body/jit(_take)/gather | solution.py:133
  275.6 4.4 %gather_fusion.5 = bf16[8,512,64]{2,1,0:T(8,128)(2,1)} fusion(bf16[48,512,64]{2,1,0:T(8,128)(2,1)} %get-tuple-element.518, s32[1024]{0:T(1024)S(1)} %pad_clamp_fusion.15), kind=kCustom, calls=%fused_computation.5.clone.clone.1 | custom fusion | bytes 1048608 | tf_op jit(solution)/shard_map/while/body/jit(_take)/gather | solution.py:127
  282.3 6.2 %fusion.170 = f32[8,512,128]{2,1,0:T(8,128)} fusion(f32[8,512]{1,0:T(8,128)S(1)} %get-tuple-element.481, f32[8,512]{1,0:T(8,128)S(1)} %get-tuple-element.482, pred[8]{0:T(512)(128)(4,1)S(1)} %broadcast_compare_fusion.2, bf16[8,512,128]{2,1,0:T(8,128)(2,1)} %gather_fusion.4, bf16[8,512,64]{2,1,0:T(8,128)(2,1)} %gather_fusion.5, ...), kind=kOutput, calls=%fused_computation.37.clone.1 | convolution fusion | flops 821035008 | bytes 4227096 | tf_op jit(solution)/shard_map/while/body/vmap()/dot_general | solution.py:35
  288.5 3.3 scatter_fusion
  294.6 4.5 %gather_fusion.4 = bf16[8,512,128]{2,1,0:T(8,128)(2,1)} fusion(bf16[48,512,128]{2,1,0:T(8,128)(2,1)} %get-tuple-element.519, s32[1024]{0:T(1024)S(1)} %pad_clamp_fusion.15), kind=kCustom, calls=%fused_computation.6.clone.clone.1 | custom fusion | bytes 2097184 | tf_op jit(solution)/shard_map/while/body/jit(_take)/gather | solution.py:133
  299.1 4.4 %gather_fusion.5 = bf16[8,512,64]{2,1,0:T(8,128)(2,1)} fusion(bf16[48,512,64]{2,1,0:T(8,128)(2,1)} %get-tuple-element.518, s32[1024]{0:T(1024)S(1)} %pad_clamp_fusion.15), kind=kCustom, calls=%fused_computation.5.clone.clone.1 | custom fusion | bytes 1048608 | tf_op jit(solution)/shard_map/while/body/jit(_take)/gather | solution.py:127
  305.8 6.2 %fusion.170 = f32[8,512,128]{2,1,0:T(8,128)} fusion(f32[8,512]{1,0:T(8,128)S(1)} %get-tuple-element.481, f32[8,512]{1,0:T(8,128)S(1)} %get-tuple-element.482, pred[8]{0:T(512)(128)(4,1)S(1)} %broadcast_compare_fusion.2, bf16[8,512,128]{2,1,0:T(8,128)(2,1)} %gather_fusion.4, bf16[8,512,64]{2,1,0:T(8,128)(2,1)} %gather_fusion.5, ...), kind=kOutput, calls=%fused_computation.37.clone.1 | convolution fusion | flops 821035008 | bytes 4227096 | tf_op jit(solution)/shard_map/while/body/vmap()/dot_general | solution.py:35
  312.0 3.3 scatter_fusion
  318.1 4.5 %gather_fusion.4 = bf16[8,512,128]{2,1,0:T(8,128)(2,1)} fusion(bf16[48,512,128]{2,1,0:T(8,128)(2,1)} %get-tuple-element.519, s32[1024]{0:T(1024)S(1)} %pad_clamp_fusion.15), kind=kCustom, calls=%fused_computation.6.clone.clone.1 | custom fusion | bytes 2097184 | tf_op jit(solution)/shard_map/while/body/jit(_take)/gather | solution.py:133
  322.6 4.4 %gather_fusion.5 = bf16[8,512,64]{2,1,0:T(8,128)(2,1)} fusion(bf16[48,512,64]{2,1,0:T(8,128)(2,1)} %get-tuple-element.518, s32[1024]{0:T(1024)S(1)} %pad_clamp_fusion.15), kind=kCustom, calls=%fused_computation.5.clone.clone.1 | custom fusion | bytes 1048608 | tf_op jit(solution)/shard_map/while/body/jit(_take)/gather | solution.py:127
  329.3 6.2 %fusion.170 = f32[8,512,128]{2,1,0:T(8,128)} fusion(f32[8,512]{1,0:T(8,128)S(1)} %get-tuple-element.481, f32[8,512]{1,0:T(8,128)S(1)} %get-tuple-element.482, pred[8]{0:T(512)(128)(4,1)S(1)} %broadcast_compare_fusion.2, bf16[8,512,128]{2,1,0:T(8,128)(2,1)} %gather_fusion.4, bf16[8,512,64]{2,1,0:T(8,128)(2,1)} %gather_fusion.5, ...), kind=kOutput, calls=%fused_computation.37.clone.1 | convolution fusion | flops 821035008 | bytes 4227096 | tf_op jit(solution)/shard_map/while/body/vmap()/dot_general | solution.py:35
  335.5 3.3 scatter_fusion
  341.6 4.5 %gather_fusion.4 = bf16[8,512,128]{2,1,0:T(8,128)(2,1)} fusion(bf16[48,512,128]{2,1,0:T(8,128)(2,1)} %get-tuple-element.519, s32[1024]{0:T(1024)S(1)} %pad_clamp_fusion.15), kind=kCustom, calls=%fused_computation.6.clone.clone.1 | custom fusion | bytes 2097184 | tf_op jit(solution)/shard_map/while/body/jit(_take)/gather | solution.py:133
  346.1 4.4 %gather_fusion.5 = bf16[8,512,64]{2,1,0:T(8,128)(2,1)} fusion(bf16[48,512,64]{2,1,0:T(8,128)(2,1)} %get-tuple-element.518, s32[1024]{0:T(1024)S(1)} %pad_clamp_fusion.15), kind=kCustom, calls=%fused_computation.5.clone.clone.1 | custom fusion | bytes 1048608 | tf_op jit(solution)/shard_map/while/body/jit(_take)/gather | solution.py:127
  352.8 6.2 %fusion.170 = f32[8,512,128]{2,1,0:T(8,128)} fusion(f32[8,512]{1,0:T(8,128)S(1)} %get-tuple-element.481, f32[8,512]{1,0:T(8,128)S(1)} %get-tuple-element.482, pred[8]{0:T(512)(128)(4,1)S(1)} %broadcast_compare_fusion.2, bf16[8,512,128]{2,1,0:T(8,128)(2,1)} %gather_fusion.4, bf16[8,512,64]{2,1,0:T(8,128)(2,1)} %gather_fusion.5, ...), kind=kOutput, calls=%fused_computation.37.clone.1 | convolution fusion | flops 821035008 | bytes 4227096 | tf_op jit(solution)/shard_map/while/body/vmap()/dot_general | solution.py:35
  359.0 3.3 scatter_fusion
  365.1 4.5 %gather_fusion.4 = bf16[8,512,128]{2,1,0:T(8,128)(2,1)} fusion(bf16[48,512,128]{2,1,0:T(8,128)(2,1)} %get-tuple-element.519, s32[1024]{0:T(1024)S(1)} %pad_clamp_fusion.15), kind=kCustom, calls=%fused_computation.6.clone.clone.1 | custom fusion | bytes 2097184 | tf_op jit(solution)/shard_map/while/body/jit(_take)/gather | solution.py:133
  369.6 4.4 %gather_fusion.5 = bf16[8,512,64]{2,1,0:T(8,128)(2,1)} fusion(bf16[48,512,64]{2,1,0:T(8,128)(2,1)} %get-tuple-element.518, s32[1024]{0:T(1024)S(1)} %pad_clamp_fusion.15), kind=kCustom, calls=%fused_computation.5.clone.clone.1 | custom fusion | bytes 1048608 | tf_op jit(solution)/shard_map/while/body/jit(_take)/gather | solution.py:127
  376.3 6.2 %fusion.170 = f32[8,512,128]{2,1,0:T(8,128)} fusion(f32[8,512]{1,0:T(8,128)S(1)} %get-tuple-element.481, f32[8,512]{1,0:T(8,128)S(1)} %get-tuple-element.482, pred[8]{0:T(512)(128)(4,1)S(1)} %broadcast_compare_fusion.2, bf16[8,512,128]{2,1,0:T(8,128)(2,1)} %gather_fusion.4, bf16[8,512,64]{2,1,0:T(8,128)(2,1)} %gather_fusion.5, ...), kind=kOutput, calls=%fused_computation.37.clone.1 | convolution fusion | flops 821035008 | bytes 4227096 | tf_op jit(solution)/shard_map/while/body/vmap()/dot_general | solution.py:35
  382.5 3.3 scatter_fusion
  388.6 4.5 %gather_fusion.4 = bf16[8,512,128]{2,1,0:T(8,128)(2,1)} fusion(bf16[48,512,128]{2,1,0:T(8,128)(2,1)} %get-tuple-element.519, s32[1024]{0:T(1024)S(1)} %pad_clamp_fusion.15), kind=kCustom, calls=%fused_computation.6.clone.clone.1 | custom fusion | bytes 2097184 | tf_op jit(solution)/shard_map/while/body/jit(_take)/gather | solution.py:133
  393.1 4.4 %gather_fusion.5 = bf16[8,512,64]{2,1,0:T(8,128)(2,1)} fusion(bf16[48,512,64]{2,1,0:T(8,128)(2,1)} %get-tuple-element.518, s32[1024]{0:T(1024)S(1)} %pad_clamp_fusion.15), kind=kCustom, calls=%fused_computation.5.clone.clone.1 | custom fusion | bytes 1048608 | tf_op jit(solution)/shard_map/while/body/jit(_take)/gather | solution.py:127
  399.9 6.2 %fusion.170 = f32[8,512,128]{2,1,0:T(8,128)} fusion(f32[8,512]{1,0:T(8,128)S(1)} %get-tuple-element.481, f32[8,512]{1,0:T(8,128)S(1)} %get-tuple-element.482, pred[8]{0:T(512)(128)(4,1)S(1)} %broadcast_compare_fusion.2, bf16[8,512,128]{2,1,0:T(8,128)(2,1)} %gather_fusion.4, bf16[8,512,64]{2,1,0:T(8,128)(2,1)} %gather_fusion.5, ...), kind=kOutput, calls=%fused_computation.37.clone.1 | convolution fusion | flops 821035008 | bytes 4227096 | tf_op jit(solution)/shard_map/while/body/vmap()/dot_general | solution.py:35
  406.0 3.3 scatter_fusion
  (401 shorter events, 109.3 us)
Async XLA Ops:
  7.2 138.1 %all-gather.3.cloned.1.call-start = ((), (), s32[]{:S(2)}) async-start(), calls=%async_computation | async-start | bytes 5242880 | tf_op jit(solution)/shard_map/all_gather | solution.py:97
  10.2 14.3 %copy-start.6 = (s32[8,128]{1,0:T(8,128)S(1)}, s32[8,128]{1,0:T(8,128)}, u32[]{:S(2)}) copy-start(s32[8,128]{1,0:T(8,128)} %param.18) | copy-start | bytes 12292
  24.3 129.7 %all-gather.5.cloned.1.call-start = ((), (), s32[]{:S(2)}) async-start(), calls=%async_computation.1 | async-start | bytes 5242880 | tf_op jit(solution)/shard_map/all_gather | solution.py:98
  24.4 4.0 copy-start.29
  24.5 3.8 copy-start.16
  39.4 9.2 %copy-start.1 = (bf16[2,256,64]{2,1,0:T(8,128)(2,1)}, bf16[2,256,64]{2,1,0:T(8,128)(2,1)S(1)}, u32[]{:S(2)}) copy-start(bf16[2,256,64]{2,1,0:T(8,128)(2,1)S(1)} %broadcast_select_fusion.5) | copy-start | bytes 196612
  44.3 3.5 copy-start.7
  45.0 31.7 %collective-permute-start.5 = (bf16[128,64]{1,0:T(8,128)(2,1)}, bf16[128,64]{1,0:T(8,128)(2,1)}, u32[]{:S(2)}, u32[]{:S(2)}) collective-permute-start(bf16[128,64]{1,0:T(8,128)(2,1)} %fusion.116), channel_id=1, source_target_pairs={{0,1},{1,0},{2,3},{3,2},{4,5},{5,4},{6,7},{7,6},{8,9},{9,8},{10,11... | collective-permute-start | bytes 49160 | tf_op jit(solution)/shard_map/ppermute | solution.py:21
  47.9 0.7 copy-start.4
  61.5 1.9 copy-start
  61.5 1.9 copy-start.3
  63.4 4.9 %copy-start.30 = (pred[4]{0:T(512)(128)(4,1)S(1)}, pred[4]{0:T(512)(128)(4,1)}, u32[]{:S(2)}) copy-start(pred[4]{0:T(512)(128)(4,1)} %copy-done.29) | copy-start | bytes 16
  63.4 5.1 %copy-start.5 = (bf16[4,128,64]{1,2,0:T(8,128)(2,1)S(1)}, bf16[4,128,64]{1,2,0:T(8,128)(2,1)}, u32[]{:S(2)}) copy-start(bf16[4,128,64]{1,2,0:T(8,128)(2,1)} %copy.47) | copy-start | bytes 196612
  63.4 5.1 %copy-start.19 = (f32[4,256]{1,0:T(4,128)S(1)}, f32[4,256]{1,0:T(4,128)}, u32[]{:S(2)}) copy-start(f32[4,256]{1,0:T(4,128)} %add.841) | copy-start | bytes 12292
  64.5 7.1 %copy-start.17 = (pred[2]{0:T(512)(128)(4,1)S(1)}, pred[2]{0:T(512)(128)(4,1)}, u32[]{:S(2)}) copy-start(pred[2]{0:T(512)(128)(4,1)} %copy-done.16) | copy-start | bytes 10
  64.5 7.2 %copy-start.2 = (bf16[2,256,64]{2,1,0:T(8,128)(2,1)S(1)}, bf16[2,256,64]{2,1,0:T(8,128)(2,1)}, u32[]{:S(2)}) copy-start(bf16[2,256,64]{2,1,0:T(8,128)(2,1)} %copy-done.1) | copy-start | bytes 196612
  64.5 9.0 %copy-start.8 = (pred[128]{0:T(512)(128)(4,1)S(1)}, pred[128]{0:T(512)(128)(4,1)}, u32[]{:S(2)}) copy-start(pred[128]{0:T(512)(128)(4,1)} %copy-done.7) | copy-start | bytes 388
  64.6 9.1 %copy-start.31 = (f32[256]{0:T(256)S(1)}, f32[256]{0:T(256)}, u32[]{:S(2)}) copy-start(f32[256]{0:T(256)} %get-tuple-element.326) | copy-start | bytes 3076
  68.2 6.7 %copy-start.28 = (s32[128]{0:T(128)S(1)}, s32[128]{0:T(128)}, u32[]{:S(2)}) copy-start(s32[128]{0:T(128)} %get-tuple-element.349) | copy-start | bytes 1540
  68.3 6.7 %copy-start.27 = (s32[128]{0:T(128)S(1)}, s32[128]{0:T(128)}, u32[]{:S(2)}) copy-start(s32[128]{0:T(128)} %get-tuple-element.347) | copy-start | bytes 1540
  68.3 6.7 %copy-start.26 = (s32[128]{0:T(128)S(1)}, s32[128]{0:T(128)}, u32[]{:S(2)}) copy-start(s32[128]{0:T(128)} %get-tuple-element.345) | copy-start | bytes 1540
  68.3 6.7 %copy-start.25 = (s32[128]{0:T(128)S(1)}, s32[128]{0:T(128)}, u32[]{:S(2)}) copy-start(s32[128]{0:T(128)} %get-tuple-element.343) | copy-start | bytes 1540
  68.3 6.7 %copy-start.24 = (s32[128]{0:T(128)S(1)}, s32[128]{0:T(128)}, u32[]{:S(2)}) copy-start(s32[128]{0:T(128)} %get-tuple-element.341) | copy-start | bytes 1540
  68.3 6.7 %copy-start.23 = (s32[128]{0:T(128)S(1)}, s32[128]{0:T(128)}, u32[]{:S(2)}) copy-start(s32[128]{0:T(128)} %get-tuple-element.339) | copy-start | bytes 1540
  68.3 6.7 %copy-start.22 = (s32[128]{0:T(128)S(1)}, s32[128]{0:T(128)}, u32[]{:S(2)}) copy-start(s32[128]{0:T(128)} %get-tuple-element.352) | copy-start | bytes 1540
  68.3 6.8 %copy-start.32 = (s32[8]{0:T(128)S(1)}, s32[8]{0:T(128)}, u32[]{:S(2)}) copy-start(s32[8]{0:T(128)} %param.17) | copy-start | bytes 100
  68.3 7.6 %copy-start.18 = (s32[8,12]{1,0:T(8,128)S(1)}, s32[8,12]{1,0:T(8,128)}, u32[]{:S(2)}) copy-start(s32[8,12]{1,0:T(8,128)} %param.16) | copy-start | bytes 1156
  68.3 7.6 %copy-start.21 = (s32[128]{0:T(128)S(1)}, s32[128]{0:T(128)}, u32[]{:S(2)}) copy-start(s32[128]{0:T(128)} %get-tuple-element.309) | copy-start | bytes 1540
  68.5 9.8 %copy-start.15 = (pred[128]{0:T(512)(128)(4,1)S(1)}, pred[128]{0:T(512)(128)(4,1)}, u32[]{:S(2)}) copy-start(pred[128]{0:T(512)(128)(4,1)} %get-tuple-element.348) | copy-start | bytes 388
  68.9 16.2 %copy-start.14 = (pred[128]{0:T(512)(128)(4,1)S(1)}, pred[128]{0:T(512)(128)(4,1)}, u32[]{:S(2)}) copy-start(pred[128]{0:T(512)(128)(4,1)} %get-tuple-element.346) | copy-start | bytes 388
  69.6 18.0 %copy-start.13 = (pred[128]{0:T(512)(128)(4,1)S(1)}, pred[128]{0:T(512)(128)(4,1)}, u32[]{:S(2)}) copy-start(pred[128]{0:T(512)(128)(4,1)} %get-tuple-element.344) | copy-start | bytes 388
  71.5 21.6 %copy-start.12 = (pred[128]{0:T(512)(128)(4,1)S(1)}, pred[128]{0:T(512)(128)(4,1)}, u32[]{:S(2)}) copy-start(pred[128]{0:T(512)(128)(4,1)} %get-tuple-element.342) | copy-start | bytes 388
  74.0 27.0 %copy-start.11 = (pred[128]{0:T(512)(128)(4,1)S(1)}, pred[128]{0:T(512)(128)(4,1)}, u32[]{:S(2)}) copy-start(pred[128]{0:T(512)(128)(4,1)} %get-tuple-element.340) | copy-start | bytes 388
  74.3 21.3 %collective-permute-start.4 = (f32[128,128]{1,0:T(8,128)S(1)}, f32[128,128]{1,0:T(8,128)S(1)}, u32[]{:S(2)}, u32[]{:S(2)}) collective-permute-start(f32[128,128]{1,0:T(8,128)S(1)} %fusion.78), channel_id=1, source_target_pairs={{0,1},{1,0},{2,3},{3,2},{4,5},{5,4},{6,7},{7,6},{8,9},{9,8},{10,11... | collective-permute-start | bytes 196616 | tf_op jit(solution)/shard_map/ppermute | solution.py:21
  74.9 31.3 %copy-start.10 = (pred[128]{0:T(512)(128)(4,1)S(1)}, pred[128]{0:T(512)(128)(4,1)}, u32[]{:S(2)}) copy-start(pred[128]{0:T(512)(128)(4,1)} %get-tuple-element.338) | copy-start | bytes 388
  78.3 33.7 %copy-start.9 = (pred[128]{0:T(512)(128)(4,1)S(1)}, pred[128]{0:T(512)(128)(4,1)}, u32[]{:S(2)}) copy-start(pred[128]{0:T(512)(128)(4,1)} %get-tuple-element.351) | copy-start | bytes 388
  78.7 5.5 %collective-permute-start.7 = (bf16[128,64]{1,0:T(8,128)(2,1)S(1)}, bf16[128,64]{1,0:T(8,128)(2,1)S(1)}, u32[]{:S(2)}, u32[]{:S(2)}) collective-permute-start(bf16[128,64]{1,0:T(8,128)(2,1)S(1)} %fusion.117), channel_id=1, source_target_pairs={{0,2},{1,3},{2,0},{3,1},{4,6},{5,7},{6,4},{7,5},{8,10},{9,11},{10,... | collective-permute-start | bytes 49160 | tf_op jit(solution)/shard_map/ppermute | solution.py:21
  85.4 1.3 collective-permute-start.9
  88.0 4.2 collective-permute-start.11
  93.2 7.0 %collective-permute-start.13 = (bf16[128,64]{1,0:T(8,128)(2,1)S(1)}, bf16[128,64]{1,0:T(8,128)(2,1)S(1)}, u32[]{:S(2)}, u32[]{:S(2)}) collective-permute-start(bf16[128,64]{1,0:T(8,128)(2,1)S(1)} %fusion.120), channel_id=1, source_target_pairs={{0,16},{4,20},{8,24},{12,28},{16,0},{20,4},{24,8},{28,12},{32,48},... | collective-permute-start | bytes 49160 | tf_op jit(solution)/shard_map/ppermute | solution.py:21
  96.5 21.2 %collective-permute-start.6 = (f32[128,128]{1,0:T(8,128)S(1)}, f32[128,128]{1,0:T(8,128)S(1)}, u32[]{:S(2)}, u32[]{:S(2)}) collective-permute-start(f32[128,128]{1,0:T(8,128)S(1)} %select_add_fusion.7), channel_id=1, source_target_pairs={{0,2},{1,3},{2,0},{3,1},{4,6},{5,7},{6,4},{7,5},{8,10},{9,11},{10,... | collective-permute-start | bytes 196616 | tf_op jit(solution)/shard_map/ppermute | solution.py:21
  101.4 4.0 collective-permute-start.15
  106.3 4.9 %collective-permute-start.17 = (bf16[128,64]{1,0:T(8,128)(2,1)S(1)}, bf16[128,64]{1,0:T(8,128)(2,1)S(1)}, u32[]{:S(2)}, u32[]{:S(2)}) collective-permute-start(bf16[128,64]{1,0:T(8,128)(2,1)S(1)} %fusion.122), channel_id=1, source_target_pairs={{0,64},{4,68},{8,72},{12,76},{16,80},{20,84},{24,88},{28,92},{32,9... | collective-permute-start | bytes 49160 | tf_op jit(solution)/shard_map/ppermute | solution.py:21
  112.1 15.7 %collective-permute-start.19 = (bf16[128,64]{1,0:T(8,128)(2,1)S(1)}, bf16[128,64]{1,0:T(8,128)(2,1)S(1)}, u32[]{:S(2)}, u32[]{:S(2)}) collective-permute-start(bf16[128,64]{1,0:T(8,128)(2,1)S(1)} %fusion.123), channel_id=1, source_target_pairs={{0,128},{4,132},{8,136},{12,140},{16,144},{20,148},{24,152},{28,15... | collective-permute-start | bytes 49160 | tf_op jit(solution)/shard_map/ppermute | solution.py:21
  117.7 22.3 %copy-start.20 = (pred[128]{0:T(512)(128)(4,1)S(1)}, pred[128]{0:T(512)(128)(4,1)}, u32[]{:S(2)}) copy-start(pred[128]{0:T(512)(128)(4,1)} %get-tuple-element.308) | copy-start | bytes 388
  118.7 1.3 collective-permute-start.8
  121.0 4.4 %collective-permute-start.10 = (f32[128,128]{1,0:T(8,128)S(1)}, f32[128,128]{1,0:T(8,128)S(1)}, u32[]{:S(2)}, u32[]{:S(2)}) collective-permute-start(f32[128,128]{1,0:T(8,128)S(1)} %select_add_fusion.5), channel_id=1, source_target_pairs={{0,8},{4,12},{8,0},{12,4},{16,24},{20,28},{24,16},{28,20},{32,40},... | collective-permute-start | bytes 196616 | tf_op jit(solution)/shard_map/ppermute | solution.py:21
  126.3 5.9 %collective-permute-start.12 = (f32[128,128]{1,0:T(8,128)S(1)}, f32[128,128]{1,0:T(8,128)S(1)}, u32[]{:S(2)}, u32[]{:S(2)}) collective-permute-start(f32[128,128]{1,0:T(8,128)S(1)} %select_add_fusion.4), channel_id=1, source_target_pairs={{0,16},{4,20},{8,24},{12,28},{16,0},{20,4},{24,8},{28,12},{32,48},... | collective-permute-start | bytes 196616 | tf_op jit(solution)/shard_map/ppermute | solution.py:21
  133.1 4.4 %collective-permute-start.14 = (f32[128,128]{1,0:T(8,128)S(1)}, f32[128,128]{1,0:T(8,128)S(1)}, u32[]{:S(2)}, u32[]{:S(2)}) collective-permute-start(f32[128,128]{1,0:T(8,128)S(1)} %select_add_fusion.3), channel_id=1, source_target_pairs={{0,32},{4,36},{8,40},{12,44},{16,48},{20,52},{24,56},{28,60},{32,0... | collective-permute-start | bytes 196616 | tf_op jit(solution)/shard_map/ppermute | solution.py:21
  138.4 5.4 %collective-permute-start.16 = (f32[128,128]{1,0:T(8,128)S(1)}, f32[128,128]{1,0:T(8,128)S(1)}, u32[]{:S(2)}, u32[]{:S(2)}) collective-permute-start(f32[128,128]{1,0:T(8,128)S(1)} %select_add_fusion.2), channel_id=1, source_target_pairs={{0,64},{4,68},{8,72},{12,76},{16,80},{20,84},{24,88},{28,92},{32,9... | collective-permute-start | bytes 196616 | tf_op jit(solution)/shard_map/ppermute | solution.py:21
  144.7 18.5 %collective-permute-start.18 = (f32[128,128]{1,0:T(8,128)S(1)}, f32[128,128]{1,0:T(8,128)S(1)}, u32[]{:S(2)}, u32[]{:S(2)}) collective-permute-start(f32[128,128]{1,0:T(8,128)S(1)} %select_add_fusion.1), channel_id=1, source_target_pairs={{0,128},{4,132},{8,136},{12,140},{16,144},{20,148},{24,152},{28,15... | collective-permute-start | bytes 196616 | tf_op jit(solution)/shard_map/ppermute | solution.py:21
  148.1 16.6 %collective-permute-start = (bf16[4096,64]{0,1:T(8,128)(2,1)}, bf16[4096,64]{0,1:T(8,128)(2,1)S(1)}, u32[]{:S(2)}, u32[]{:S(2)}) collective-permute-start(bf16[4096,64]{0,1:T(8,128)(2,1)} %copy.41), channel_id=1, source_target_pairs={{0,4},{4,8},{8,12},{12,16},{16,20},{20,24},{24,28},{28,32},{32,36}... | collective-permute-start | bytes 1572872 | tf_op jit(solution)/shard_map/ppermute | solution.py:14
  150.4 14.8 %collective-permute-start.1 = (bf16[4096,64]{0,1:T(8,128)(2,1)S(1)}, bf16[4096,64]{0,1:T(8,128)(2,1)}, u32[]{:S(2)}, u32[]{:S(2)}) collective-permute-start(bf16[4096,64]{0,1:T(8,128)(2,1)S(1)} %copy.42), channel_id=1, source_target_pairs={{4,0},{8,4},{12,8},{16,12},{20,16},{24,20},{28,24},{32,28},{36,32}... | collective-permute-start | bytes 1572872 | tf_op jit(solution)/shard_map/ppermute | solution.py:15
  157.1 31.7 %collective-permute-start.2 = (bf16[4096,128]{1,0:T(8,128)(2,1)}, bf16[4096,128]{1,0:T(8,128)(2,1)}, u32[]{:S(2)}, u32[]{:S(2)}) collective-permute-start(bf16[4096,128]{1,0:T(8,128)(2,1)} %get-tuple-element.334), channel_id=1, source_target_pairs={{0,4},{4,8},{8,12},{12,16},{16,20},{20,24},{24,28},{28,32},{32,36}... | collective-permute-start | bytes 3145736 | tf_op jit(solution)/shard_map/ppermute | solution.py:14
  159.2 29.6 %collective-permute-start.3 = (bf16[4096,128]{1,0:T(8,128)(2,1)}, bf16[4096,128]{1,0:T(8,128)(2,1)}, u32[]{:S(2)}, u32[]{:S(2)}) collective-permute-start(bf16[4096,128]{1,0:T(8,128)(2,1)} %get-tuple-element.335), channel_id=1, source_target_pairs={{4,0},{8,4},{12,8},{16,12},{20,16},{24,20},{28,24},{32,28},{36,32}... | collective-permute-start | bytes 3145736 | tf_op jit(solution)/shard_map/ppermute | solution.py:15
Sparse Core Ops, SparseCore 0:
  24.5 53.5 all-gather.2
  79.9 52.7 all-gather.4
where the time goes:
time: 425 us; the launch traced here: 418 us
  local copies, waits for them, and re-layouts  186 us (44%)
  other arithmetic  86 us (20%)
  matrix products  65.6 us (15%)
  starting transfers between devices  37.6 us (9%)
  waiting for transfers between devices  25.6 us (6%)
  between operations  16.5 us (4%)
    dot_general x9, matrix products, apply_tiles(): return jnp.dot(weights, source_rows, preferred_element_type=jnp.float32)  55.6 us
    gather x9, local copies, waits for them, and re-layouts, add_own(): jnp.take(around_probes, targets, axis=0)  40.7 us
    gather x9, local copies, waits for them, and re-layouts, add_own(): jnp.take(around_points, targets, axis=0)  39.9 us
    scatter-add x9, other arithmetic, add_own(): running.at[owner_block]  29.7 us
    reduce_sum x23, other arithmetic, row_squares(): return jnp.sum(jnp.square(values.astype(jnp.float32)), axis=-1)  27.3 us
    ppermute x16, starting transfers between devices, partner(): lax.ppermute(shard, axis, [(i, i ^ 1 << distance) for i in range(lax.axis...  26.2 us
    ppermute x16, waiting for transfers between devices, partner(): lax.ppermute(shard, axis, [(i, i ^ 1 << distance) for i in range(lax.axis...  25.6 us
    gather x13, local copies, waits for them, and re-layouts, condense(): return (picked, jnp.take(samples, chosen, axis=0) + mixed_part / totals)  23.3 us
  transfers between devices with their start and end apart: 22, of which 10 were waited for; matrix products, arithmetic and copies ran while one was open for 24% of the time, Pallas kernels for 0%

commit v1 on v0

v1 whole, which is shorter than its diff:
```python
import functools

import jax
import jax.numpy as jnp
from jax import lax
from jax.experimental import pallas as pl
from jax.experimental.pallas import tpu as pltpu
from jax.sharding import PartitionSpec as P

MESH = pl.DeviceIdType.MESH
BF16 = jnp.bfloat16
F32 = jnp.float32
LANES = 128
LEAF = 512
DIM = 64
BLK = 8
HALF = 4
SKEL = 128
RING = 8
LOG2E = 1.4426950408889634
SCALE = 2.0 * LOG2E / DIM


def dot(a, b):
    return jnp.dot(a, b, preferred_element_type=F32)


def dot_nt(a, b):
    return lax.dot_general(a, b, (((1,), (1,)), ((), ())), preferred_element_type=F32)


def split3(h):
    h1 = h.astype(BF16).astype(F32)
    h2 = (h - h1).astype(BF16).astype(F32)
    h3 = (h - h1 - h2).astype(BF16).astype(F32)
    return h1, h2, h3


def one_hot(row, width):
    col = jnp.transpose(jnp.broadcast_to(row, (LANES, LANES)))
    lane = lax.broadcasted_iota(jnp.int32, (LANES, LANES), 1)
    parts = [
        jnp.where(col == lane + j * LANES, 1.0, 0.0).astype(BF16)
        for j in range(width // LANES)
    ]
    return jnp.concatenate(parts, axis=1)


def with_ones(picked):
    lane = lax.broadcasted_iota(jnp.int32, picked.shape, 1)
    return jnp.where((lane >= DIM) & (lane < DIM + 3), 1.0, picked).astype(BF16)


def weigh(picked, coords):
    return jnp.exp2(dot_nt(with_ones(picked), coords) * SCALE)


def hi_lo(x):
    hi = x.astype(BF16)
    return hi, (x - hi.astype(F32)).astype(BF16)


def merge(both, chosen):
    rows = dot(one_hot(chosen, 2 * SKEL), both)
    picked = rows[:, :LANES]
    weights = weigh(picked, both[:, :LANES])
    totals = jnp.sum(weights, axis=1, keepdims=True)
    high, low = hi_lo(weights)
    mixed = dot(high, both[:, LANES:])
    mixed = mixed[:, :LANES] + mixed[:, LANES:] + dot(low, both[:, LANES : 2 * LANES])
    samples = rows[:, LANES : 2 * LANES] + rows[:, 2 * LANES :] + mixed / totals
    s_hi, s_lo = hi_lo(samples)
    return jnp.concatenate([picked.astype(BF16), s_hi, s_lo], axis=1), samples


def gather_kernel(
    leaf_count,
    points_ref,
    probes_ref,
    order_ref,
    sets_ref,
    merge_ref,
    probes_hbm,
    win_t,
    win_q,
    own_a,
    root_ref,
    own_t,
    own_c,
    nodes,
    pairs,
    tree,
    final,
    copy_sem,
    own_send,
    own_recv,
    fwd_send,
    fwd_recv,
    edge_send,
    edge_recv,
    tree_send,
    tree_recv,
):
    leaf = lax.axis_index("leaf")
    y = lax.axis_index("sub")
    rank = leaf * 4 + y
    first_block = rank * BLK
    plus = (leaf, lax.rem(y + 1, 4))
    minus = (leaf, lax.rem(y + 3, 4))
    up = (lax.rem(leaf + 1, leaf_count), y)
    down = (lax.rem(leaf + leaf_count - 1, leaf_count), y)
    levels = [("sub", d) for d in (1, 2)]
    d = 1
    while d < leaf_count:
        levels.append(("leaf", d))
        d *= 2

    def other(axis, dist):
        place = y if axis == "sub" else leaf
        bit = lax.rem(place // dist, 2)
        there = place + dist - 2 * dist * bit
        return bit, ((leaf, there) if axis == "sub" else (there, y))

    greet = [plus, minus, (leaf, lax.rem(y + 2, 4)), up, down]
    greet += [other(axis, dist)[1] for axis, dist in levels if axis == "leaf" and dist > 1]
    barrier = pltpu.get_barrier_semaphore()
    for who in greet:
        pl.semaphore_signal(barrier, inc=1, device_id=who, device_id_type=MESH)
    pl.semaphore_wait(barrier, len(greet))

    wins = (win_t, win_q)
    owns = (own_t, probes_hbm)

    def remote(src, dst, send, recv, who):
        return pltpu.make_async_remote_copy(
            src_ref=src, dst_ref=dst, send_sem=send, recv_sem=recv, device_id=who, device_id_type=MESH
        )

    def own_copy(kind, way, piece):
        at = (piece if way == 0 else 1 - piece) * HALF
        return remote(
            owns[kind].at[pl.ds(at, HALF)],
            wins[kind].at[pl.ds(BLK + y * BLK + at, HALF)],
            own_send.at[kind, way, piece],
            own_recv.at[kind, way, piece],
            plus if way == 0 else minus,
        )

    def fwd_copy(kind, way, j):
        src_y = lax.rem(y + 3, 4) if way == 0 else lax.rem(y + 1, 4)
        at = BLK + src_y * BLK + way * HALF + j
        ref = wins[kind].at[pl.ds(at, 1)]
        return remote(
            ref, ref, fwd_send.at[kind, way, j], fwd_recv.at[kind, way, j], plus if way == 0 else minus
        )

    def edge_copy(kind, side, j, own):
        at = (3 * BLK if side == 0 else 0) + j
        src = owns[kind].at[pl.ds(j, 1)] if own else wins[kind].at[pl.ds(BLK + at, 1)]
        return remote(
            src,
            wins[kind].at[pl.ds((0 if side == 0 else 5 * BLK) + j, 1)],
            edge_send.at[kind, side, j],
            edge_recv.at[kind, side, j],
            up if side == 0 else down,
        )

    has = (leaf < leaf_count - 1, leaf > 0)

    def start_edges(kind, j_from, j_to, prev_when, next_when, own=False):
        for side, cond in ((0, prev_when), (1, next_when)):

            @pl.when(cond & has[side])
            def _(side=side):
                def body(j, carry):
                    edge_copy(kind, side, j, own).start()
                    return carry

                lax.fori_loop(j_from, j_to, body, 0)

    for way in range(2):
        own_copy(1, way, 0).start()
    start_edges(1, 0, BLK, y == 3, y == 0, own=True)
    keep_q = pltpu.make_async_copy(probes_hbm, win_q.at[pl.ds(BLK + y * BLK, BLK)], copy_sem.at[1])
    keep_q.start()

    lane = lax.broadcasted_iota(jnp.int32, (LANES, LANES), 1)

    def permute(b, carry):
        pts = points_ref[pl.ds(b * LEAF, LEAF), :]
        pts = jnp.concatenate([pts, jnp.zeros((LEAF, LANES - DIM), BF16)], axis=1)
        for q in range(LEAF // LANES):
            hot = one_hot(order_ref[pl.ds(b * 4 + q, 1), :], LEAF)
            rows = dot(hot, pts)
            h1, h2, h3 = split3(-0.5 * jnp.sum(rows * rows, axis=1, keepdims=True))
            form = jnp.where(lane == DIM, h1, jnp.where(lane == DIM + 1, h2, jnp.where(lane == DIM + 2, h3, rows)))
            own_c[b, q * LANES : (q + 1) * LANES, :] = form.astype(BF16)
            ones = jnp.where((lane >= DIM + 3) & (lane < DIM + 6), 1.0, form)
            own_a[b, q * LANES : (q + 1) * LANES, :] = ones.astype(BF16)
            own_t[b, :, q * LANES : (q + 1) * LANES] = jnp.transpose(rows)[:DIM].astype(BF16)
        return carry

    lax.fori_loop(0, BLK, permute, 0)
    for way in range(2):
        own_copy(0, way, 0).start()
    start_edges(0, 0, BLK, y == 3, y == 0, own=True)
    keep_t = pltpu.make_async_copy(own_t, win_t.at[pl.ds(BLK + y * BLK, BLK)], copy_sem.at[0])
    keep_t.start()

    def leaf_node(b, carry):
        coords = own_c[b]
        probe = probes_ref[b]
        hot = one_hot(sets_ref[pl.ds(b, 1), :], LEAF)
        picked = dot(hot, coords)
        weights = weigh(picked, coords)
        totals = jnp.sum(weights, axis=1, keepdims=True)
        high, low = hi_lo(weights)
        samples = dot(hot, probe) + (dot(high, probe) + dot(low, probe)) / totals
        s_hi, s_lo = hi_lo(samples)
        nodes[pl.ds(pl.multiple_of(b * SKEL, SKEL), SKEL), :] = jnp.concatenate(
            [picked.astype(BF16), s_hi, s_lo], axis=1
        )
        return carry

    lax.fori_loop(0, BLK, leaf_node, 0)
    for way in range(2):
        for kind in range(2):
            own_copy(kind, way, 1).start()

    bit, _ = other(*levels[0])
    for k in range(4):
        chosen = merge_ref[pl.ds(first_block + 2 * k, 1), :]
        pairs[k * SKEL : (k + 1) * SKEL, :] = merge(nodes[2 * k * SKEL : 2 * (k + 1) * SKEL, :], chosen)[0]
    two = [
        merge(pairs[2 * k * SKEL : 2 * (k + 1) * SKEL, :], merge_ref[pl.ds(first_block + 4 * k + 1, 1), :])[0]
        for k in range(2)
    ]
    for k in range(2):
        nodes[k * SKEL : (k + 1) * SKEL, :] = two[k]
    node, samples = merge(nodes[: 2 * SKEL, :], merge_ref[pl.ds(first_block + 3, 1), :])

    def level(i, node):
        axis, dist = levels[i]
        bit, who = other(axis, dist)
        mine = pl.ds(pl.multiple_of(bit * SKEL, SKEL), SKEL)
        tree[i, mine, :] = node
        copy = remote(tree.at[i, mine], tree.at[i, mine], tree_send.at[i], tree_recv.at[i], who)
        copy.start()
        span = BLK * dist if axis == "sub" else BLK * 4 * dist
        first = first_block // (2 * span) * (2 * span)
        chosen = merge_ref[pl.ds(first + span - 1, 1), :]
        copy.wait()
        return merge(tree[i], chosen)

    near_prev = (y == 0) | (y == 2)
    near_next = (y == 1) | (y == 3)
    far_prev = y == 1
    far_next = y == 2
    from_minus = (y == 0, y == 1)
    from_plus = (y == 2, y == 3)

    node, samples = level(0, node)
    node, samples = level(1, node)
    for kind in (1, 0):
        for way in range(2):
            own_copy(kind, way, 0).wait_recv()

            def send_on(j, carry, kind=kind, way=way):
                fwd_copy(kind, way, j).start()
                return carry

            lax.fori_loop(0, HALF, send_on, 0)
        start_edges(kind, 0, HALF, *from_minus)
        start_edges(kind, HALF, BLK, *from_plus)
    half_way = 2 + (len(levels) - 2) // 2
    for i in range(2, half_way):
        node, samples = level(i, node)
    for kind in (1, 0):
        for way in range(2):
            own_copy(kind, way, 1).wait_recv()
        start_edges(kind, HALF, BLK, *from_minus)
        start_edges(kind, 0, HALF, *from_plus)
    for i in range(half_way, len(levels)):
        node, samples = level(i, node)
    final[...] = samples
    row = final[pl.ds(rank // 2, 1), :] if leaf_count == 64 else final[pl.ds(0, 1), :]
    odd = lax.rem(rank, 2) == 1
    row = jnp.broadcast_to(row, (8, LANES))
    root_ref[...] = jnp.where(odd, pltpu.roll(row, DIM, 1), row)

    def far(j, carry):
        for way in range(2):
            for kind in (1, 0):
                fwd_copy(kind, way, j).wait_recv()
                for side, cond in ((0, far_prev), (1, far_next)):

                    @pl.when(cond & has[side])
                    def _(side=side, kind=kind, way=way):
                        edge_copy(kind, side, way * HALF + j, False).start()

        return carry

    lax.fori_loop(0, HALF, far, 0)

    for kind in range(2):
        for way in range(2):
            for piece in range(2):
                own_copy(kind, way, piece).wait_send()

    def drain(j, carry):
        for kind in range(2):
            for way in range(2):
                fwd_copy(kind, way, j).wait_send()
        return carry

    lax.fori_loop(0, HALF, drain, 0)
    for side in range(2):

        @pl.when(has[side])
        def _(side=side):
            def body(j, carry):
                for kind in range(2):
                    edge_copy(kind, side, j, False).wait_send()
                return carry

            lax.fori_loop(0, BLK, body, 0)

        @pl.when(has[1 - side])
        def _(side=side):
            def body(j, carry):
                for kind in range(2):
                    edge_copy(kind, side, j, False).wait_recv()
                return carry

            lax.fori_loop(0, BLK, body, 0)

    keep_q.wait()
    keep_t.wait()


def near_kernel(
    lists_ref, counts_ref, own_a, win_t, win_q, out_ref, flat, ring_t, ring_q, acc, outs, sem_t, sem_q, sem_o
):
    start = lax.axis_index("leaf") * 32 - BLK

    def flatten(g, total):
        def one(s, carry):
            flat[total + s] = lists_ref[g, s] - start
            return carry

        count = counts_ref[g]
        lax.fori_loop(0, count, one, 0)
        return total + count

    total = lax.fori_loop(0, BLK, flatten, 0)

    def fetch(t):
        slot = lax.rem(t, RING)
        c = flat[t]
        return (
            pltpu.make_async_copy(win_t.at[c], ring_t.at[slot, pl.ds(0, DIM)], sem_t.at[slot]),
            pltpu.make_async_copy(win_q.at[c], ring_q.at[slot], sem_q.at[slot]),
        )

    def begin(t, carry):
        for copy in fetch(t):
            copy.start()
        return carry

    lax.fori_loop(0, jnp.minimum(total, RING - 1), begin, 0)
    for slot in range(RING):
        ring_t[slot, DIM:, :] = jnp.zeros((LANES - DIM, LEAF), BF16)
    row_id = lax.broadcasted_iota(jnp.int32, (16, LEAF), 0)

    def block(g, t0):
        acc[...] = jnp.zeros_like(acc)

        def pair(s, carry):
            t = t0 + s
            slot = lax.rem(t, RING)

            @pl.when(t + RING - 1 < total)
            def _():
                for copy in fetch(t + RING - 1):
                    copy.start()

            for copy in fetch(t):
                copy.wait()
            pts = ring_t[slot, :DIM, :].astype(F32)
            h1, h2, h3 = split3(-0.5 * jnp.sum(pts * pts, axis=0, keepdims=True))
            tail = jnp.where(row_id < 3, 1.0, 0.0)
            tail = jnp.where(row_id == 3, h1, jnp.where(row_id == 4, h2, jnp.where(row_id == 5, h3, tail)))
            ring_t[slot, DIM : DIM + 16, :] = tail.astype(BF16)
            source = ring_t[slot]
            probe = ring_q[slot]
            for q in range(LEAF // LANES):
                rows = slice(q * LANES, (q + 1) * LANES)
                weights = jnp.exp2(dot(own_a[g, rows, :], source) * SCALE).astype(BF16)
                acc[rows, :] += dot(weights, probe)
            return carry

        count = counts_ref[g]
        lax.fori_loop(0, count, pair, 0)
        which = lax.rem(g, 2)
        done = pltpu.make_async_copy(outs.at[which], out_ref.at[g], sem_o.at[which])

        @pl.when(g >= 2)
        def _():
            done.wait()

        outs[which] = acc[...] * (LEAF**-0.5)
        done.start()
        return t0 + count

    lax.fori_loop(0, BLK, block, 0)
    for g in (BLK - 2, BLK - 1):
        pltpu.make_async_copy(outs.at[g % 2], out_ref.at[g], sem_o.at[g % 2]).wait()


def on_device(points, probes, order, near_lists, near_counts, leaf_sets, merge_sets):
    leaf_count = lax.axis_size("leaf")
    vmem = pl.BlockSpec(memory_space=pltpu.VMEM)
    hbm = pl.BlockSpec(memory_space=pltpu.HBM)
    smem = pl.BlockSpec(memory_space=pltpu.SMEM)
    window = 6 * BLK
    level_count = 2 + leaf_count.bit_length() - 1
    probe_blocks = probes.reshape(BLK, LEAF, LANES)
    dma = pltpu.SemaphoreType.DMA
    win_t, win_q, own_a, root = pl.pallas_call(
        functools.partial(gather_kernel, leaf_count),
        out_shape=(
            jax.ShapeDtypeStruct((window, DIM, LEAF), BF16),
            jax.ShapeDtypeStruct((window, LEAF, LANES), BF16),
            jax.ShapeDtypeStruct((BLK, LEAF, LANES), BF16),
            jax.ShapeDtypeStruct((8, LANES), F32),
        ),
        in_specs=[vmem, vmem, vmem, vmem, vmem, hbm],
        out_specs=(hbm, hbm, vmem, vmem),
        scratch_shapes=[
            pltpu.VMEM((BLK, DIM, LEAF), BF16),
            pltpu.VMEM((BLK, LEAF, LANES), BF16),
            pltpu.VMEM((BLK * SKEL, 3 * LANES), BF16),
            pltpu.VMEM((BLK // 2 * SKEL, 3 * LANES), BF16),
            pltpu.VMEM((level_count, 2 * SKEL, 3 * LANES), BF16),
            pltpu.VMEM((SKEL, LANES), F32),
            dma((2,)),
            dma((2, 2, 2)),
            dma((2, 2, 2)),
            dma((2, 2, HALF)),
            dma((2, 2, HALF)),
            dma((2, 2, BLK)),
            dma((2, 2, BLK)),
            dma((level_count,)),
            dma((level_count,)),
        ],
        compiler_params=pltpu.CompilerParams(
            collective_id=0, has_side_effects=True, vmem_limit_bytes=40 * 2**20
        ),
        name="gather_and_tree",
    )(points, probe_blocks, order.reshape(-1, LANES), leaf_sets, merge_sets, probe_blocks)
    near = pl.pallas_call(
        near_kernel,
        out_shape=jax.ShapeDtypeStruct((BLK, LEAF, LANES), F32),
        in_specs=[smem, smem, vmem, hbm, hbm],
        out_specs=hbm,
        scratch_shapes=[
            pltpu.SMEM((128,), jnp.int32),
            pltpu.VMEM((RING, LANES, LEAF), BF16),
            pltpu.VMEM((RING, LEAF, LANES), BF16),
            pltpu.VMEM((LEAF, LANES), F32),
            pltpu.VMEM((2, LEAF, LANES), F32),
            dma((RING,)),
            dma((RING,)),
            dma((2,)),
        ],
        compiler_params=pltpu.CompilerParams(vmem_limit_bytes=40 * 2**20),
        name="near_field",
    )(near_lists, near_counts, own_a, win_t, win_q)
    return near.reshape(BLK * LEAF, LANES), root[0, :DIM]


def solution(mesh):
    both = P(("leaf", "sub"), None)
    in_specs = (both, both, P(("leaf", "sub")), both, P(("leaf", "sub")), both, P())
    out_specs = (both, P(("leaf", "sub")))
    return jax.shard_map(on_device, mesh=mesh, in_specs=in_specs, out_specs=out_specs, check_vma=False)
```

time: 425 us -> 182 us (0.43)
  the two profiles are of different devices: /device:TPU:66 before, /device:TPU:48 now
where the time goes in v1:
time: 182 us
  Pallas kernels  175 us (96%)
  local copies, waits for them, and re-layouts  5.9 us (3%)
    pallas_call x1, Pallas kernels, on_device(): pl.pallas_call(functools.partial(gather_kernel, leaf_count), out_shape=(j...  97 us
    pallas_call x1, Pallas kernels, on_device(): pl.pallas_call(near_kernel, out_shape=jax.ShapeDtypeStruct((BLK, LEAF, LA...  78 us
    unnamed x13, local copies, waits for them, and re-layouts  5.39 us

profile of v1, /device:TPU:48, one launch (start us, length us, event | category | flops | bytes accessed | tf_op | source)
XLA Modules:
  0.0 181.6 jit_solution(592709841018073633)
XLA Ops:
  0.6 0.0 copy-start.5
  0.6 0.0 copy-start.4
  0.6 1.5 copy.9.points_ref
  2.2 0.0 copy-start
  2.2 1.2 copy-done
  3.4 0.0 copy-start.1
  3.4 1.2 copy-done.1
  4.6 0.0 copy-start.2
  4.6 0.7 copy-done.2
  5.4 0.0 copy-start.3
  5.4 0.7 copy-done.3
  6.0 97.0 %gather_and_tree.1 = (bf16[48,64,512]{2,1,0:T(8,128)(2,1)S(1)}, bf16[48,512,128]{2,1,0:T(8,128)(2,1)S(1)}, bf16[8,512,128]{2,1,0:T(8,128)(2,1)S(1)}, f32[8,128]{1,0:T(8,128)S(1)}) custom-call(bf16[4096,64]{1,0:T(8,128)(2,1)S(1)} %copy.9.points_ref, bf16[8,512,128]{2,1,0:T(8,128)(2,1)S(1)} %bitcast.5, s32[32,128]{1,0:T(8,128)S(1)} %bitcast.7, ...), custom_call_target="tpu_custom_call" | custom-call | tf_op jit(solution)/shard_map/gather_and_tree/pallas_call | solution.py:429
  103.1 0.0 copy-done.5
  103.1 0.0 copy-done.4
  103.1 78.0 %near_field.1 = f32[8,512,128]{2,1,0:T(8,128)} custom-call(s32[8,12]{1,0:T(8,128)S(1)} %copy-done.4, s32[8]{0:T(128)S(1)} %copy-done.5, bf16[8,512,128]{2,1,0:T(8,128)(2,1)S(1)} %get-tuple-element.6.own_a, bf16[48,64,512]{2,1,0:T(8,128)(2,1)S(1)} %get-tuple-element.7.win_t, bf16[48,512,128]{2,1,0:T(8,128)(2,1)S(1)} %get-tuple-element.8.win_q), custom_call_target="tpu_custom_call" | custom-call | tf_op jit(solution)/shard_map/near_field/pallas_call | solution.py:461
  181.1 0.5 slice_bitcast_fusion
Async XLA Ops:
  0.6 102.4 %copy-start.5 = (s32[8]{0:T(128)S(1)}, s32[8]{0:T(128)}, u32[]{:S(2)}) copy-start(s32[8]{0:T(128)} %counts_ref.1) | copy-start | bytes 100
  0.6 102.4 %copy-start.4 = (s32[8,12]{1,0:T(8,128)S(1)}, s32[8,12]{1,0:T(8,128)}, u32[]{:S(2)}) copy-start(s32[8,12]{1,0:T(8,128)} %lists_ref.1) | copy-start | bytes 1156
  2.2 1.2 copy-start
  3.4 1.2 copy-start.1
  4.6 0.7 copy-start.2
  5.4 0.7 copy-start.3

commit v2 on v1

v2 whole, which is shorter than its diff:
```python
import functools

import jax
import jax.numpy as jnp
from jax import lax
from jax.experimental import pallas as pl
from jax.experimental.pallas import tpu as pltpu
from jax.sharding import PartitionSpec as P

MESH = pl.DeviceIdType.MESH
BF16 = jnp.bfloat16
F32 = jnp.float32
LANES = 128
LEAF = 512
DIM = 64
FORM = DIM + 16
BLK = 8
HALF = 4
SKEL = 128
NODE = FORM + 2 * SKEL
PAIRS = 4
LOG2E = 1.4426950408889634
SCALE = 2.0 * LOG2E / DIM


def dot(a, b):
    return jnp.dot(a, b, preferred_element_type=F32)


def dot_tn(a, b):
    return lax.dot_general(a, b, (((0,), (0,)), ((), ())), preferred_element_type=F32)


def half_squares(coords):
    h = -0.5 * jnp.sum(coords * coords, axis=0, keepdims=True)
    h1 = h.astype(BF16).astype(F32)
    h2 = (h - h1).astype(BF16).astype(F32)
    h3 = (h - h1 - h2).astype(BF16).astype(F32)
    return h1, h2, h3


def tail_rows(squares, first, ones):
    shape = (FORM - DIM, squares[0].shape[1])
    row = lax.broadcasted_iota(jnp.int32, shape, 0)
    tail = jnp.zeros(shape, F32)
    if ones is not None:
        tail = jnp.where((row >= ones) & (row < ones + 3), 1.0, tail)
    for i, part in enumerate(squares):
        tail = jnp.where(row == first + i, part, tail)
    return tail.astype(BF16)


def one_hot(row, height):
    shape = (height, row.shape[1])
    return jnp.where(lax.broadcasted_iota(jnp.int32, shape, 0) == row, 1.0, 0.0).astype(BF16)


def weigh(picked, coords):
    row = lax.broadcasted_iota(jnp.int32, picked.shape, 0)
    left = jnp.where((row >= DIM) & (row < DIM + 3), 1.0, picked).astype(BF16)
    return jnp.exp2(dot_tn(left, coords) * SCALE)


def hi_lo(x):
    hi = x.astype(BF16)
    return hi, (x - hi.astype(F32)).astype(BF16)


def node_of(picked, samples):
    return jnp.concatenate([picked.astype(BF16), *hi_lo(samples)], axis=0)


def merge(left, right, chosen):
    coords = jnp.concatenate([left[:FORM], right[:FORM]], axis=1)
    high = jnp.concatenate([left[FORM : FORM + SKEL], right[FORM : FORM + SKEL]], axis=0)
    low = jnp.concatenate([left[FORM + SKEL :], right[FORM + SKEL :]], axis=0)
    both = jnp.concatenate([high, low], axis=1)
    hot = one_hot(chosen, 2 * SKEL)
    picked = dot(coords, hot)
    kept = dot_tn(hot, both)
    weights = weigh(picked, coords)
    totals = jnp.sum(weights, axis=1, keepdims=True)
    w_hi, w_lo = hi_lo(weights)
    mixed = dot(w_hi, both)
    mixed = mixed[:, :LANES] + mixed[:, LANES:] + dot(w_lo, high)
    samples = kept[:, :LANES] + kept[:, LANES:] + mixed / totals
    return picked, samples


def gather_kernel(
    leaf_count,
    points_hbm,
    probes_hbm,
    order_hbm,
    sets_hbm,
    merge_hbm,
    win_t,
    win_q,
    root_ref,
    points,
    order,
    sets,
    chosen_rows,
    own_h,
    nodes,
    tree,
    final,
    in_sem,
    row_sem,
    own_send,
    own_recv,
    fwd_send,
    fwd_recv,
    edge_send,
    edge_recv,
    tree_send,
    tree_recv,
):
    leaf = lax.axis_index("leaf")
    y = lax.axis_index("sub")
    rank = leaf * 4 + y
    first_block = rank * BLK
    mine = BLK + y * BLK
    plus = (leaf, lax.rem(y + 1, 4))
    minus = (leaf, lax.rem(y + 3, 4))
    up = (lax.rem(leaf + 1, leaf_count), y)
    down = (lax.rem(leaf + leaf_count - 1, leaf_count), y)
    levels = [("sub", d) for d in (1, 2)]
    d = 1
    while d < leaf_count:
        levels.append(("leaf", d))
        d *= 2

    def other(axis, dist):
        place = y if axis == "sub" else leaf
        bit = lax.rem(place // dist, 2)
        there = place + dist - 2 * dist * bit
        return bit, ((leaf, there) if axis == "sub" else (there, y))

    inputs = [
        pltpu.make_async_copy(order_hbm, order, in_sem.at[0]),
        pltpu.make_async_copy(points_hbm, points, in_sem.at[1]),
        pltpu.make_async_copy(sets_hbm, sets, in_sem.at[2]),
        pltpu.make_async_copy(probes_hbm, win_q.at[pl.ds(mine, BLK)], in_sem.at[3]),
    ]
    wanted = [first_block + i for i in range(7)]
    for axis, dist in levels:
        span = BLK * dist if axis == "sub" else BLK * 4 * dist
        wanted.append(first_block // (2 * span) * (2 * span) + span - 1)
    rows = [
        pltpu.make_async_copy(merge_hbm.at[pl.ds(w, 1)], chosen_rows.at[pl.ds(i, 1)], row_sem.at[i])
        for i, w in enumerate(wanted)
    ]
    for copy in inputs + rows:
        copy.start()

    greet = [plus, minus, (leaf, lax.rem(y + 2, 4)), up, down]
    greet += [other(axis, dist)[1] for axis, dist in levels if axis == "leaf" and dist > 1]
    barrier = pltpu.get_barrier_semaphore()
    for who in greet:
        pl.semaphore_signal(barrier, inc=1, device_id=who, device_id_type=MESH)
    pl.semaphore_wait(barrier, len(greet))

    wins = (win_t, win_q)

    def remote(src, dst, send, recv, who):
        return pltpu.make_async_remote_copy(
            src_ref=src, dst_ref=dst, send_sem=send, recv_sem=recv, device_id=who, device_id_type=MESH
        )

    def own_copy(kind, way, piece):
        at = (piece if way == 0 else 1 - piece) * HALF
        there = wins[kind].at[pl.ds(mine + at, HALF)]
        return remote(
            probes_hbm.at[pl.ds(at, HALF)] if kind else there,
            there,
            own_send.at[kind, way, piece],
            own_recv.at[kind, way, piece],
            plus if way == 0 else minus,
        )

    def fwd_copy(kind, way, j):
        src_y = lax.rem(y + 3, 4) if way == 0 else lax.rem(y + 1, 4)
        ref = wins[kind].at[pl.ds(BLK + src_y * BLK + way * HALF + j, 1)]
        return remote(
            ref, ref, fwd_send.at[kind, way, j], fwd_recv.at[kind, way, j], plus if way == 0 else minus
        )

    def edge_copy(kind, side, j, own=False):
        at = BLK + (3 * BLK if side == 0 else 0) + j
        src = probes_hbm.at[pl.ds(j, 1)] if own and kind else wins[kind].at[pl.ds(at, 1)]
        return remote(
            src,
            wins[kind].at[pl.ds((0 if side == 0 else 5 * BLK) + j, 1)],
            edge_send.at[kind, side, j],
            edge_recv.at[kind, side, j],
            up if side == 0 else down,
        )

    has = (leaf < leaf_count - 1, leaf > 0)

    def start_edges(kind, j_from, j_to, prev_when, next_when, own=False):
        for side, cond in ((0, prev_when), (1, next_when)):

            @pl.when(cond & has[side])
            def _(side=side):
                def body(j, carry):
                    edge_copy(kind, side, j, own).start()
                    return carry

                lax.fori_loop(j_from, j_to, body, 0)

    for way in range(2):
        own_copy(1, way, 0).start()
    start_edges(1, 0, BLK, y == 3, y == 0, own=True)

    inputs[0].wait()
    inputs[1].wait()

    def permute(i, carry):
        for k in range(2):
            b = 2 * i + k
            to = jnp.concatenate([order[pl.ds(b * 4 + q, 1), :] for q in range(4)], axis=1)
            at = pl.ds(pl.multiple_of(b * LEAF, LEAF), LEAF)
            coords = dot(points[:, at], one_hot(to, LEAF))
            win_t[mine + b] = coords.astype(BF16)
            own_h[b] = tail_rows(half_squares(coords), 0, None)
        return carry

    lax.fori_loop(0, BLK // 2, permute, 0)
    for way in range(2):
        own_copy(0, way, 0).start()
    start_edges(0, 0, BLK, y == 3, y == 0, own=True)

    inputs[2].wait()
    inputs[3].wait()

    def leaf_nodes(i, carry):
        for k in range(4):
            b = 4 * i + k
            coords = jnp.concatenate([win_t[mine + b], own_h[b]], axis=0)
            probe = win_q[mine + b]
            hot = one_hot(sets[pl.ds(b, 1), :], LEAF)
            picked = dot(coords, hot)
            kept = dot_tn(hot, probe)
            weights = weigh(picked, coords)
            totals = jnp.sum(weights, axis=1, keepdims=True)
            w_hi, w_lo = hi_lo(weights)
            samples = kept + (dot(w_hi, probe) + dot(w_lo, probe)) / totals
            nodes[b] = node_of(picked, samples)
        return carry

    lax.fori_loop(0, BLK // 4, leaf_nodes, 0)
    for way in range(2):
        own_copy(1, way, 1).start()
    for copy in rows:
        copy.wait()

    def row(i):
        return chosen_rows[i : i + 1, :]

    def merge_all(count, first, step):
        out = [node_of(*merge(nodes[2 * k], nodes[2 * k + 1], row(first + step * k))) for k in range(count)]
        for k in range(count):
            nodes[k] = out[k]

    merge_all(4, 0, 2)
    merge_all(2, 1, 4)
    picked, samples = merge(nodes[0], nodes[1], row(3))

    def level(i, picked, samples):
        axis, dist = levels[i]
        bit, who = other(axis, dist)
        tree[i, bit] = node_of(picked, samples)
        ref = tree.at[i, bit]
        copy = remote(ref, ref, tree_send.at[i], tree_recv.at[i], who)
        copy.start()
        copy.wait()
        return merge(tree[i, 0], tree[i, 1], row(7 + i))

    far_prev = y == 1
    far_next = y == 2
    from_minus = (y == 0, y == 1)
    from_plus = (y == 2, y == 3)

    for i in range(2):
        picked, samples = level(i, picked, samples)
    for kind in (1, 0):
        for way in range(2):
            own_copy(kind, way, 0).wait_recv()

            def send_on(j, carry, kind=kind, way=way):
                fwd_copy(kind, way, j).start()
                return carry

            lax.fori_loop(0, HALF, send_on, 0)
        start_edges(kind, 0, HALF, *from_minus)
        start_edges(kind, HALF, BLK, *from_plus)
    for way in range(2):
        own_copy(0, way, 1).start()
    half_way = 2 + (len(levels) - 2) * 2 // 3
    for i in range(2, half_way):
        picked, samples = level(i, picked, samples)
    for kind in (1, 0):
        for way in range(2):
            own_copy(kind, way, 1).wait_recv()
        start_edges(kind, HALF, BLK, *from_minus)
        start_edges(kind, 0, HALF, *from_plus)
    for i in range(half_way, len(levels)):
        picked, samples = level(i, picked, samples)
    final[...] = samples
    last = final[pl.ds(rank // 2 if leaf_count == 64 else 0, 1), :]
    last = jnp.broadcast_to(last, (8, LANES))
    root_ref[...] = jnp.where(lax.rem(rank, 2) == 1, pltpu.roll(last, DIM, 1), last)

    def far(j, carry):
        for way in range(2):
            for kind in (1, 0):
                fwd_copy(kind, way, j).wait_recv()
                for side, cond in ((0, far_prev), (1, far_next)):

                    @pl.when(cond & has[side])
                    def _(side=side, kind=kind, way=way):
                        edge_copy(kind, side, way * HALF + j).start()

        return carry

    lax.fori_loop(0, HALF, far, 0)

    for kind in range(2):
        for way in range(2):
            for piece in range(2):
                own_copy(kind, way, piece).wait_send()

    def drain(j, carry):
        for kind in range(2):
            for way in range(2):
                fwd_copy(kind, way, j).wait_send()
        return carry

    lax.fori_loop(0, HALF, drain, 0)
    for side in range(2):

        @pl.when(has[side])
        def _(side=side):
            def body(j, carry):
                for kind in range(2):
                    edge_copy(kind, side, j).wait_send()
                return carry

            lax.fori_loop(0, BLK, body, 0)

        @pl.when(has[1 - side])
        def _(side=side):
            def body(j, carry):
                for kind in range(2):
                    edge_copy(kind, side, j).wait_recv()
                return carry

            lax.fori_loop(0, BLK, body, 0)


def near_kernel(lists_ref, counts_ref, win_t, win_q, out_ref, flat_g, flat_c, acc, outs, sem_o):
    start = lax.axis_index("leaf") * 32 - BLK
    mine = BLK + lax.axis_index("sub") * BLK

    def flatten(g, total):
        def one(s, carry):
            flat_g[total + s] = g
            flat_c[total + s] = lists_ref[g, s] - start
            return carry

        count = counts_ref[g]
        lax.fori_loop(0, count, one, 0)
        return total + count

    total = lax.fori_loop(0, BLK, flatten, 0)
    for i in range(PAIRS - 1):
        flat_g[total + i] = BLK
        flat_c[total + i] = mine
    acc[...] = jnp.zeros_like(acc)

    def step(i, carry):
        for k in range(PAIRS):
            g = flat_g[i * PAIRS + k]
            c = flat_c[i * PAIRS + k]
            target = win_t[mine + jnp.minimum(g, BLK - 1)]
            source = win_t[c]
            left = jnp.concatenate([target, tail_rows(half_squares(target.astype(F32)), 0, 3)], axis=0)
            right = jnp.concatenate([source, tail_rows(half_squares(source.astype(F32)), 3, 0)], axis=0)
            weights = jnp.exp2(dot_tn(left, right) * SCALE).astype(BF16)
            acc[g] += dot(weights, win_q[c])
        return carry

    lax.fori_loop(0, (total + PAIRS - 1) // PAIRS, step, 0)
    for g in range(BLK):
        outs[g] = acc[g] * (LEAF**-0.5)
        pltpu.make_async_copy(outs.at[g], out_ref.at[g], sem_o.at[g]).start()
    for g in range(BLK):
        pltpu.make_async_copy(outs.at[g], out_ref.at[g], sem_o.at[g]).wait()


def in_hbm(x):
    return pltpu.with_memory_space_constraint(x, pltpu.HBM)


def on_device(points, probes, order, near_lists, near_counts, leaf_sets, merge_sets):
    leaf_count = lax.axis_size("leaf")
    vmem = pl.BlockSpec(memory_space=pltpu.VMEM)
    hbm = pl.BlockSpec(memory_space=pltpu.HBM)
    smem = pl.BlockSpec(memory_space=pltpu.SMEM)
    window = 6 * BLK
    level_count = 2 + leaf_count.bit_length() - 1
    dma = pltpu.SemaphoreType.DMA
    win_t, win_q, root = pl.pallas_call(
        functools.partial(gather_kernel, leaf_count),
        out_shape=(
            jax.ShapeDtypeStruct((window, DIM, LEAF), BF16),
            jax.ShapeDtypeStruct((window, LEAF, LANES), BF16),
            jax.ShapeDtypeStruct((8, LANES), F32),
        ),
        in_specs=[hbm] * 5,
        out_specs=(vmem, vmem, vmem),
        scratch_shapes=[
            pltpu.VMEM((DIM, BLK * LEAF), BF16),
            pltpu.VMEM((BLK * LEAF // LANES, LANES), jnp.int32),
            pltpu.VMEM((BLK, SKEL), jnp.int32),
            pltpu.VMEM((16, SKEL), jnp.int32),
            pltpu.VMEM((BLK, FORM - DIM, LEAF), BF16),
            pltpu.VMEM((BLK, NODE, LANES), BF16),
            pltpu.VMEM((level_count, 2, NODE, LANES), BF16),
            pltpu.VMEM((SKEL, LANES), F32),
            dma((4,)),
            dma((7 + level_count,)),
            dma((2, 2, 2)),
            dma((2, 2, 2)),
            dma((2, 2, HALF)),
            dma((2, 2, HALF)),
            dma((2, 2, BLK)),
            dma((2, 2, BLK)),
            dma((level_count,)),
            dma((level_count,)),
        ],
        compiler_params=pltpu.CompilerParams(
            collective_id=0, has_side_effects=True, vmem_limit_bytes=32 * 2**20
        ),
        name="gather_and_tree",
    )(*map(in_hbm, (points.T, probes.reshape(BLK, LEAF, LANES), order.reshape(-1, LANES), leaf_sets, merge_sets)))
    near = pl.pallas_call(
        near_kernel,
        out_shape=jax.ShapeDtypeStruct((BLK, LEAF, LANES), F32),
        in_specs=[smem, smem, vmem, vmem],
        out_specs=hbm,
        scratch_shapes=[
            pltpu.SMEM((128,), jnp.int32),
            pltpu.SMEM((128,), jnp.int32),
            pltpu.VMEM((BLK + 1, LEAF, LANES), F32),
            pltpu.VMEM((BLK, LEAF, LANES), F32),
            dma((BLK,)),
        ],
        compiler_params=pltpu.CompilerParams(vmem_limit_bytes=32 * 2**20),
        name="near_field",
    )(in_hbm(near_lists), in_hbm(near_counts), win_t, win_q)
    return near.reshape(BLK * LEAF, LANES), root[0, :DIM]


def solution(mesh):
    both = P(("leaf", "sub"), None)
    in_specs = (both, both, P(("leaf", "sub")), both, P(("leaf", "sub")), both, P())
    out_specs = (both, P(("leaf", "sub")))
    return jax.shard_map(on_device, mesh=mesh, in_specs=in_specs, out_specs=out_specs, check_vma=False)
```

time: 182 us -> 120 us (0.66)
  the two profiles are of different devices: /device:TPU:48 before, /device:TPU:19 now
where the time goes in v2:
time: 120 us
  Pallas kernels  119 us (99%)
    pallas_call x1, Pallas kernels, on_device(): pl.pallas_call(functools.partial(gather_kernel, leaf_count), out_shape=(j...  101 us
    pallas_call x1, Pallas kernels, on_device(): pl.pallas_call(near_kernel, out_shape=jax.ShapeDtypeStruct((BLK, LEAF, LA...  18.3 us

profile of v2, /device:TPU:19, one launch (start us, length us, event | category | flops | bytes accessed | tf_op | source)
XLA Modules:
  0.0 120.1 jit_solution(6922864446555432100)
XLA Ops:
  0.6 100.6 %gather_and_tree.1 = (bf16[48,64,512]{2,1,0:T(8,128)(2,1)S(1)}, bf16[48,512,128]{2,1,0:T(8,128)(2,1)S(1)}, f32[8,128]{1,0:T(8,128)S(1)}) custom-call(bf16[64,4096]{1,0:T(8,128)(2,1)} %bitcast.8, bf16[8,512,128]{2,1,0:T(8,128)(2,1)} %bitcast.7, s32[32,128]{1,0:T(8,128)} %bitcast.9, s32[8,128]{1,0:T(8,128)} %sets_hbm.1, s32[2047,128]{1,0:T(8,128)} %merge_hbm.1), custom_call_target="tpu_custom_call" | custom-call | tf_op jit(solution)/shard_map/gather_and_tree/pallas_call | solution.py:415
  101.2 18.3 %near_field.1 = f32[8,512,128]{2,1,0:T(8,128)} custom-call(s32[8,12]{1,0:T(8,128)} %lists_ref.1, s32[8]{0:T(128)} %counts_ref.1, bf16[48,64,512]{2,1,0:T(8,128)(2,1)S(1)} %get-tuple-element.5.win_t, bf16[48,512,128]{2,1,0:T(8,128)(2,1)S(1)} %get-tuple-element.6.win_q), custom_call_target="tpu_custom_call" | custom-call | tf_op jit(solution)/shard_map/near_field/pallas_call | solution.py:449
  119.6 0.5 slice_bitcast_fusion

commit v3 on v2

--- a/solution.py
+++ b/solution.py
@@ -18,7 +18,7 @@
 HALF = 4
 SKEL = 128
 NODE = FORM + 2 * SKEL
-PAIRS = 4
+PAIRS = 8
 LOG2E = 1.4426950408889634
 SCALE = 2.0 * LOG2E / DIM
 
@@ -85,6 +85,15 @@
     mixed = mixed[:, :LANES] + mixed[:, LANES:] + dot(w_lo, high)
     samples = kept[:, :LANES] + kept[:, LANES:] + mixed / totals
     return picked, samples
+
+
+def rounds_of(leaf_count):
+    rounds = [("sub", 1, 4), ("leaf", 1, 2)]
+    d = 2
+    while d < leaf_count:
+        rounds.append(("leaf", d, 4 if 4 * d <= leaf_count else 2))
+        d *= rounds[-1][2]
+    return rounds
 
 
 def gather_kernel(
@@ -109,6 +118,8 @@
     row_sem,
     own_send,
     own_recv,
+    late_send,
+    late_recv,
     fwd_send,
     fwd_recv,
     edge_send,
@@ -125,17 +136,13 @@
     minus = (leaf, lax.rem(y + 3, 4))
     up = (lax.rem(leaf + 1, leaf_count), y)
     down = (lax.rem(leaf + leaf_count - 1, leaf_count), y)
-    levels = [("sub", d) for d in (1, 2)]
-    d = 1
-    while d < leaf_count:
-        levels.append(("leaf", d))
-        d *= 2
-
-    def other(axis, dist):
+    rounds = rounds_of(leaf_count)
+
+    def partner(axis, d, n, k):
         place = y if axis == "sub" else leaf
-        bit = lax.rem(place // dist, 2)
-        there = place + dist - 2 * dist * bit
-        return bit, ((leaf, there) if axis == "sub" else (there, y))
+        me = lax.rem(place // d, n)
+        there = place + (lax.rem(me + k, n) - me) * d
+        return me, ((leaf, there) if axis == "sub" else (there, y))
 
     inputs = [
         pltpu.make_async_copy(order_hbm, order, in_sem.at[0]),
@@ -144,9 +151,12 @@
         pltpu.make_async_copy(probes_hbm, win_q.at[pl.ds(mine, BLK)], in_sem.at[3]),
     ]
     wanted = [first_block + i for i in range(7)]
-    for axis, dist in levels:
-        span = BLK * dist if axis == "sub" else BLK * 4 * dist
-        wanted.append(first_block // (2 * span) * (2 * span) + span - 1)
+    row_at = []
+    for axis, d, n in rounds:
+        span = BLK * d if axis == "sub" else BLK * 4 * d
+        first = first_block // (n * span) * (n * span)
+        row_at.append(len(wanted))
+        wanted += [first + span - 1] if n == 2 else [first + span - 1, first + 3 * span - 1, first + 2 * span - 1]
     rows = [
         pltpu.make_async_copy(merge_hbm.at[pl.ds(w, 1)], chosen_rows.at[pl.ds(i, 1)], row_sem.at[i])
         for i, w in enumerate(wanted)
@@ -154,8 +164,10 @@
     for copy in inputs + rows:
         copy.start()
 
-    greet = [plus, minus, (leaf, lax.rem(y + 2, 4)), up, down]
-    greet += [other(axis, dist)[1] for axis, dist in levels if axis == "leaf" and dist > 1]
+    greet = [up, down]
+    for axis, d, n in rounds:
+        if axis == "sub" or d > 1:
+            greet += [partner(axis, d, n, k)[1] for k in range(1, n)]
     barrier = pltpu.get_barrier_semaphore()
     for who in greet:
         pl.semaphore_signal(barrier, inc=1, device_id=who, device_id_type=MESH)
@@ -168,16 +180,17 @@
             src_ref=src, dst_ref=dst, send_sem=send, recv_sem=recv, device_id=who, device_id_type=MESH
         )
 
-    def own_copy(kind, way, piece):
-        at = (piece if way == 0 else 1 - piece) * HALF
-        there = wins[kind].at[pl.ds(mine + at, HALF)]
-        return remote(
-            probes_hbm.at[pl.ds(at, HALF)] if kind else there,
-            there,
-            own_send.at[kind, way, piece],
-            own_recv.at[kind, way, piece],
-            plus if way == 0 else minus,
-        )
+    def own_piece(kind, way, at, size, send, recv):
+        there = wins[kind].at[pl.ds(mine + at, size)]
+        src = probes_hbm.at[pl.ds(at, size)] if kind else there
+        return remote(src, there, send, recv, plus if way == 0 else minus)
+
+    def early(kind, way):
+        return own_piece(kind, way, way * HALF, HALF, own_send.at[kind, way], own_recv.at[kind, way])
+
+    def late(kind, way, p):
+        at = (1 - way) * HALF + 2 * p
+        return own_piece(kind, way, at, 2, late_send.at[kind, way, p], late_recv.at[kind, way, p])
 
     def fwd_copy(kind, way, j):
         src_y = lax.rem(y + 3, 4) if way == 0 else lax.rem(y + 1, 4)
@@ -199,20 +212,21 @@
 
     has = (leaf < leaf_count - 1, leaf > 0)
 
-    def start_edges(kind, j_from, j_to, prev_when, next_when, own=False):
+    def start_edges(kinds, j_from, j_to, prev_when, next_when, own=False):
         for side, cond in ((0, prev_when), (1, next_when)):
 
             @pl.when(cond & has[side])
             def _(side=side):
                 def body(j, carry):
-                    edge_copy(kind, side, j, own).start()
+                    for kind in kinds:
+                        edge_copy(kind, side, j, own).start()
                     return carry
 
                 lax.fori_loop(j_from, j_to, body, 0)
 
     for way in range(2):
-        own_copy(1, way, 0).start()
-    start_edges(1, 0, BLK, y == 3, y == 0, own=True)
+        early(1, way).start()
+    start_edges((1,), 0, BLK, y == 3, y == 0, own=True)
 
     inputs[0].wait()
     inputs[1].wait()
@@ -229,8 +243,8 @@
 
     lax.fori_loop(0, BLK // 2, permute, 0)
     for way in range(2):
-        own_copy(0, way, 0).start()
-    start_edges(0, 0, BLK, y == 3, y == 0, own=True)
+        early(0, way).start()
+    start_edges((0,), 0, BLK, y == 3, y == 0, own=True)
 
     inputs[2].wait()
     inputs[3].wait()
@@ -251,8 +265,6 @@
         return carry
 
     lax.fori_loop(0, BLK // 4, leaf_nodes, 0)
-    for way in range(2):
-        own_copy(1, way, 1).start()
     for copy in rows:
         copy.wait()
 
@@ -266,71 +278,92 @@
 
     merge_all(4, 0, 2)
     merge_all(2, 1, 4)
-    picked, samples = merge(nodes[0], nodes[1], row(3))
-
-    def level(i, picked, samples):
-        axis, dist = levels[i]
-        bit, who = other(axis, dist)
-        tree[i, bit] = node_of(picked, samples)
-        ref = tree.at[i, bit]
-        copy = remote(ref, ref, tree_send.at[i], tree_recv.at[i], who)
-        copy.start()
-        copy.wait()
-        return merge(tree[i, 0], tree[i, 1], row(7 + i))
-
-    far_prev = y == 1
-    far_next = y == 2
+    state = merge(nodes[0], nodes[1], row(3))
+
+    def begin(i, state):
+        axis, d, n = rounds[i]
+        me, _ = partner(axis, d, n, 1)
+        ref = tree.at[i, me]
+        tree[i, me] = node_of(*state)
+        copies = [
+            remote(ref, ref, tree_send.at[i, k - 1], tree_recv.at[i, k - 1], partner(axis, d, n, k)[1])
+            for k in range(1, n)
+        ]
+        for copy in copies:
+            copy.start()
+        return copies
+
+    def finish(i, copies):
+        for copy in copies:
+            copy.wait()
+        at = row_at[i]
+        if rounds[i][2] == 2:
+            return merge(tree[i, 0], tree[i, 1], row(at))
+        low = node_of(*merge(tree[i, 0], tree[i, 1], row(at)))
+        high = node_of(*merge(tree[i, 2], tree[i, 3], row(at + 1)))
+        return merge(low, high, row(at + 2))
+
     from_minus = (y == 0, y == 1)
     from_plus = (y == 2, y == 3)
 
-    for i in range(2):
-        picked, samples = level(i, picked, samples)
+    copies = begin(0, state)
     for kind in (1, 0):
         for way in range(2):
-            own_copy(kind, way, 0).wait_recv()
-
-            def send_on(j, carry, kind=kind, way=way):
+            early(kind, way).wait_recv()
+
+    def send_on(j, carry):
+        for way in range(2):
+            for kind in (1, 0):
                 fwd_copy(kind, way, j).start()
-                return carry
-
-            lax.fori_loop(0, HALF, send_on, 0)
-        start_edges(kind, 0, HALF, *from_minus)
-        start_edges(kind, HALF, BLK, *from_plus)
-    for way in range(2):
-        own_copy(0, way, 1).start()
-    half_way = 2 + (len(levels) - 2) * 2 // 3
-    for i in range(2, half_way):
-        picked, samples = level(i, picked, samples)
-    for kind in (1, 0):
+        return carry
+
+    lax.fori_loop(0, HALF, send_on, 0)
+    start_edges((1, 0), 0, HALF, *from_minus)
+    start_edges((1, 0), HALF, BLK, *from_plus)
+    for p in range(2):
         for way in range(2):
-            own_copy(kind, way, 1).wait_recv()
-        start_edges(kind, HALF, BLK, *from_minus)
-        start_edges(kind, 0, HALF, *from_plus)
-    for i in range(half_way, len(levels)):
-        picked, samples = level(i, picked, samples)
-    final[...] = samples
-    last = final[pl.ds(rank // 2 if leaf_count == 64 else 0, 1), :]
-    last = jnp.broadcast_to(last, (8, LANES))
-    root_ref[...] = jnp.where(lax.rem(rank, 2) == 1, pltpu.roll(last, DIM, 1), last)
+            for kind in (1, 0):
+                late(kind, way, p).start()
+    state = finish(0, copies)
 
     def far(j, carry):
         for way in range(2):
             for kind in (1, 0):
                 fwd_copy(kind, way, j).wait_recv()
-                for side, cond in ((0, far_prev), (1, far_next)):
-
-                    @pl.when(cond & has[side])
-                    def _(side=side, kind=kind, way=way):
+        for side, cond in ((0, y == 1), (1, y == 2)):
+
+            @pl.when(cond & has[side])
+            def _(side=side):
+                for way in range(2):
+                    for kind in (1, 0):
                         edge_copy(kind, side, way * HALF + j).start()
 
         return carry
 
-    lax.fori_loop(0, HALF, far, 0)
+    for i in range(1, len(rounds)):
+        copies = begin(i, state)
+        if i == len(rounds) - 2:
+            lax.fori_loop(0, HALF // 2, far, 0)
+        if i == len(rounds) - 1:
+            lax.fori_loop(HALF // 2, HALF, far, 0)
+        state = finish(i, copies)
+    final[...] = state[1]
+    last = final[pl.ds(rank // 2 if leaf_count == 64 else 0, 1), :]
+    last = jnp.broadcast_to(last, (8, LANES))
+    root_ref[...] = jnp.where(lax.rem(rank, 2) == 1, pltpu.roll(last, DIM, 1), last)
+
+    for p in range(2):
+        for way in range(2):
+            for kind in (1, 0):
+                late(kind, way, p).wait_recv()
+        start_edges((1, 0), HALF + 2 * p, HALF + 2 * p + 2, *from_minus)
+        start_edges((1, 0), 2 * p, 2 * p + 2, *from_plus)
 
     for kind in range(2):
         for way in range(2):
-            for piece in range(2):
-                own_copy(kind, way, piece).wait_send()
+            early(kind, way).wait_send()
+            for p in range(2):
+                late(kind, way, p).wait_send()
 
     def drain(j, carry):
         for kind in range(2):
@@ -410,7 +443,8 @@
     hbm = pl.BlockSpec(memory_space=pltpu.HBM)
     smem = pl.BlockSpec(memory_space=pltpu.SMEM)
     window = 6 * BLK
-    level_count = 2 + leaf_count.bit_length() - 1
+    rounds = rounds_of(leaf_count)
+    row_count = 7 + sum(n - 1 for _, _, n in rounds)
     dma = pltpu.SemaphoreType.DMA
     win_t, win_q, root = pl.pallas_call(
         functools.partial(gather_kernel, leaf_count),
@@ -425,21 +459,23 @@
             pltpu.VMEM((DIM, BLK * LEAF), BF16),
             pltpu.VMEM((BLK * LEAF // LANES, LANES), jnp.int32),
             pltpu.VMEM((BLK, SKEL), jnp.int32),
-            pltpu.VMEM((16, SKEL), jnp.int32),
+            pltpu.VMEM((row_count, SKEL), jnp.int32),
             pltpu.VMEM((BLK, FORM - DIM, LEAF), BF16),
             pltpu.VMEM((BLK, NODE, LANES), BF16),
-            pltpu.VMEM((level_count, 2, NODE, LANES), BF16),
+            pltpu.VMEM((len(rounds), 4, NODE, LANES), BF16),
             pltpu.VMEM((SKEL, LANES), F32),
             dma((4,)),
-            dma((7 + level_count,)),
+            dma((row_count,)),
+            dma((2, 2)),
+            dma((2, 2)),
             dma((2, 2, 2)),
             dma((2, 2, 2)),
             dma((2, 2, HALF)),
             dma((2, 2, HALF)),
             dma((2, 2, BLK)),
             dma((2, 2, BLK)),
-            dma((level_count,)),
-            dma((level_count,)),
+            dma((len(rounds), 3)),
+            dma((len(rounds), 3)),
         ],
         compiler_params=pltpu.CompilerParams(
             collective_id=0, has_side_effects=True, vmem_limit_bytes=32 * 2**20

time: 120 us -> 94.2 us (0.79)
  the two profiles are of different devices: /device:TPU:19 before, /device:TPU:48 now
where the time goes in v3:
time: 94.2 us; the launch traced here: 92.4 us
  Pallas kernels  91.2 us (97%)
    pallas_call x1, Pallas kernels, on_device(): pl.pallas_call(functools.partial(gather_kernel, leaf_count), out_shape=(j...  71.7 us
    pallas_call x1, Pallas kernels, on_device(): pl.pallas_call(near_kernel, out_shape=jax.ShapeDtypeStruct((BLK, LEAF, LA...  19.5 us

profile of v3, /device:TPU:48, one launch (start us, length us, event | category | flops | bytes accessed | tf_op | source)
XLA Modules:
  0.0 92.4 jit_solution(7064772795891474344)
XLA Ops:
  0.6 71.7 %gather_and_tree.1 = (bf16[48,64,512]{2,1,0:T(8,128)(2,1)S(1)}, bf16[48,512,128]{2,1,0:T(8,128)(2,1)S(1)}, f32[8,128]{1,0:T(8,128)S(1)}) custom-call(bf16[64,4096]{1,0:T(8,128)(2,1)} %bitcast.8, bf16[8,512,128]{2,1,0:T(8,128)(2,1)} %bitcast.7, s32[32,128]{1,0:T(8,128)} %bitcast.9, s32[8,128]{1,0:T(8,128)} %sets_hbm.1, s32[2047,128]{1,0:T(8,128)} %merge_hbm.1), custom_call_target="tpu_custom_call" | custom-call | tf_op jit(solution)/shard_map/gather_and_tree/pallas_call | solution.py:449
  72.3 19.5 %near_field.1 = f32[8,512,128]{2,1,0:T(8,128)} custom-call(s32[8,12]{1,0:T(8,128)} %lists_ref.1, s32[8]{0:T(128)} %counts_ref.1, bf16[48,64,512]{2,1,0:T(8,128)(2,1)S(1)} %get-tuple-element.5.win_t, bf16[48,512,128]{2,1,0:T(8,128)(2,1)S(1)} %get-tuple-element.6.win_q), custom_call_target="tpu_custom_call" | custom-call | tf_op jit(solution)/shard_map/near_field/pallas_call | solution.py:485
  91.9 0.5 slice_bitcast_fusion

commit v4 on v3

--- a/solution.py
+++ b/solution.py
@@ -18,7 +18,9 @@
 HALF = 4
 SKEL = 128
 NODE = FORM + 2 * SKEL
-PAIRS = 8
+PAIRS = 4
+EARLY_STEPS = 2
+FWD_STEPS = 1
 LOG2E = 1.4426950408889634
 SCALE = 2.0 * LOG2E / DIM
 
@@ -96,8 +98,25 @@
     return rounds
 
 
+def pair_sum(target, source, probe):
+    left = jnp.concatenate([target, tail_rows(half_squares(target.astype(F32)), 0, 3)], axis=0)
+    right = jnp.concatenate([source, tail_rows(half_squares(source.astype(F32)), 3, 0)], axis=0)
+    return dot(jnp.exp2(dot_tn(left, right) * SCALE).astype(BF16), probe)
+
+
+def classify(block, shard_first, y):
+    at = block - shard_first
+    inside = (at >= 0) & (at < 4 * BLK)
+    j = at & (BLK - 1)
+    off = (lax.shift_right_arithmetic(at, 3) - y) & 3
+    early = inside & ((off == 0) | ((off == 3) & (j < HALF)) | ((off == 1) & (j >= HALF)))
+    return early, j + jnp.where(off == 0, 0, BLK), inside & (off == 2), j
+
+
 def gather_kernel(
     leaf_count,
+    lists,
+    counts,
     points_hbm,
     probes_hbm,
     order_hbm,
@@ -105,6 +124,7 @@
     merge_hbm,
     win_t,
     win_q,
+    acc,
     root_ref,
     points,
     order,
@@ -114,8 +134,14 @@
     nodes,
     tree,
     final,
+    early_t,
+    early_q,
+    fwd_t,
+    fwd_q,
+    plan,
     in_sem,
     row_sem,
+    keep_sem,
     own_send,
     own_recv,
     late_send,
@@ -131,9 +157,12 @@
     y = lax.axis_index("sub")
     rank = leaf * 4 + y
     first_block = rank * BLK
+    y_minus = lax.rem(y + 3, 4)
+    y_plus = lax.rem(y + 1, 4)
+    y_far = lax.rem(y + 2, 4)
     mine = BLK + y * BLK
-    plus = (leaf, lax.rem(y + 1, 4))
-    minus = (leaf, lax.rem(y + 3, 4))
+    plus = (leaf, y_plus)
+    minus = (leaf, y_minus)
     up = (lax.rem(leaf + 1, leaf_count), y)
     down = (lax.rem(leaf + leaf_count - 1, leaf_count), y)
     rounds = rounds_of(leaf_count)
@@ -148,7 +177,7 @@
         pltpu.make_async_copy(order_hbm, order, in_sem.at[0]),
         pltpu.make_async_copy(points_hbm, points, in_sem.at[1]),
         pltpu.make_async_copy(sets_hbm, sets, in_sem.at[2]),
-        pltpu.make_async_copy(probes_hbm, win_q.at[pl.ds(mine, BLK)], in_sem.at[3]),
+        pltpu.make_async_copy(probes_hbm, early_q.at[pl.ds(0, BLK)], in_sem.at[3]),
     ]
     wanted = [first_block + i for i in range(7)]
     row_at = []
@@ -174,34 +203,55 @@
     pl.semaphore_wait(barrier, len(greet))
 
     wins = (win_t, win_q)
+    earlies = (early_t, early_q)
+    fwds = (fwd_t, fwd_q)
 
     def remote(src, dst, send, recv, who):
         return pltpu.make_async_remote_copy(
             src_ref=src, dst_ref=dst, send_sem=send, recv_sem=recv, device_id=who, device_id_type=MESH
         )
 
-    def own_piece(kind, way, at, size, send, recv):
-        there = wins[kind].at[pl.ds(mine + at, size)]
-        src = probes_hbm.at[pl.ds(at, size)] if kind else there
-        return remote(src, there, send, recv, plus if way == 0 else minus)
+    def own(kind, at, size):
+        return (probes_hbm if kind else early_t).at[pl.ds(at, size)]
 
     def early(kind, way):
-        return own_piece(kind, way, way * HALF, HALF, own_send.at[kind, way], own_recv.at[kind, way])
-
-    def late(kind, way, p):
-        at = (1 - way) * HALF + 2 * p
-        return own_piece(kind, way, at, 2, late_send.at[kind, way, p], late_recv.at[kind, way, p])
-
-    def fwd_copy(kind, way, j):
-        src_y = lax.rem(y + 3, 4) if way == 0 else lax.rem(y + 1, 4)
-        ref = wins[kind].at[pl.ds(BLK + src_y * BLK + way * HALF + j, 1)]
         return remote(
-            ref, ref, fwd_send.at[kind, way, j], fwd_recv.at[kind, way, j], plus if way == 0 else minus
+            own(kind, way * HALF, HALF),
+            earlies[kind].at[pl.ds(BLK + way * HALF, HALF)],
+            own_send.at[kind, way],
+            own_recv.at[kind, way],
+            minus if way else plus,
         )
 
-    def edge_copy(kind, side, j, own=False):
-        at = BLK + (3 * BLK if side == 0 else 0) + j
-        src = probes_hbm.at[pl.ds(j, 1)] if own and kind else wins[kind].at[pl.ds(at, 1)]
+    def late(kind, way, j):
+        at = (1 - way) * HALF + j
+        return remote(
+            own(kind, at, 1),
+            wins[kind].at[pl.ds(mine + at, 1)],
+            late_send.at[kind, way, j],
+            late_recv.at[kind, way, j],
+            minus if way else plus,
+        )
+
+    def forward(kind, way, j):
+        at = way * HALF + j
+        return remote(
+            earlies[kind].at[pl.ds(BLK + at, 1)],
+            fwds[kind].at[pl.ds(at, 1)],
+            fwd_send.at[kind, way, j],
+            fwd_recv.at[kind, way, j],
+            minus if way else plus,
+        )
+
+    def edge_copy(kind, side, j, source):
+        if source == "own":
+            src = own(kind, j, 1)
+        elif source == "early":
+            src = earlies[kind].at[pl.ds(BLK + j, 1)]
+        elif source == "far":
+            src = fwds[kind].at[pl.ds(j, 1)]
+        else:
+            src = wins[kind].at[pl.ds(BLK + (3 * BLK if side == 0 else 0) + j, 1)]
         return remote(
             src,
             wins[kind].at[pl.ds((0 if side == 0 else 5 * BLK) + j, 1)],
@@ -212,21 +262,21 @@
 
     has = (leaf < leaf_count - 1, leaf > 0)
 
-    def start_edges(kinds, j_from, j_to, prev_when, next_when, own=False):
+    def start_edges(kinds, blocks, prev_when, next_when, source):
         for side, cond in ((0, prev_when), (1, next_when)):
 
             @pl.when(cond & has[side])
             def _(side=side):
                 def body(j, carry):
                     for kind in kinds:
-                        edge_copy(kind, side, j, own).start()
+                        edge_copy(kind, side, j, source).start()
                     return carry
 
-                lax.fori_loop(j_from, j_to, body, 0)
+                lax.fori_loop(*blocks, body, 0)
 
     for way in range(2):
         early(1, way).start()
-    start_edges((1,), 0, BLK, y == 3, y == 0, own=True)
+    start_edges((1,), (0, BLK), y == 3, y == 0, "own")
 
     inputs[0].wait()
     inputs[1].wait()
@@ -237,14 +287,14 @@
             to = jnp.concatenate([order[pl.ds(b * 4 + q, 1), :] for q in range(4)], axis=1)
             at = pl.ds(pl.multiple_of(b * LEAF, LEAF), LEAF)
             coords = dot(points[:, at], one_hot(to, LEAF))
-            win_t[mine + b] = coords.astype(BF16)
+            early_t[b] = coords.astype(BF16)
             own_h[b] = tail_rows(half_squares(coords), 0, None)
         return carry
 
     lax.fori_loop(0, BLK // 2, permute, 0)
     for way in range(2):
         early(0, way).start()
-    start_edges((0,), 0, BLK, y == 3, y == 0, own=True)
+    start_edges((0,), (0, BLK), y == 3, y == 0, "own")
 
     inputs[2].wait()
     inputs[3].wait()
@@ -252,8 +302,8 @@
     def leaf_nodes(i, carry):
         for k in range(4):
             b = 4 * i + k
-            coords = jnp.concatenate([win_t[mine + b], own_h[b]], axis=0)
-            probe = win_q[mine + b]
+            coords = jnp.concatenate([early_t[b], own_h[b]], axis=0)
+            probe = early_q[b]
             hot = one_hot(sets[pl.ds(b, 1), :], LEAF)
             picked = dot(coords, hot)
             kept = dot_tn(hot, probe)
@@ -279,6 +329,51 @@
     merge_all(4, 0, 2)
     merge_all(2, 1, 4)
     state = merge(nodes[0], nodes[1], row(3))
+
+    def plan_block(g, carry):
+        count = counts[g]
+        picks = [[g, 0] for _ in range(EARLY_STEPS)] + [[0, 0] for _ in range(FWD_STEPS)]
+        seen_e = 0
+        seen_f = 0
+        for s in range(1, lists.shape[1]):
+            is_e, at_e, is_f, at_f = classify(lists[g, s], leaf * 4 * BLK, y)
+            is_e = is_e & (s < count)
+            is_f = is_f & (s < count)
+            for i in range(EARLY_STEPS):
+                hit = is_e & (seen_e == i)
+                picks[i] = [jnp.where(hit, at_e, picks[i][0]), jnp.where(hit, 1, picks[i][1])]
+            for i in range(FWD_STEPS):
+                hit = is_f & (seen_f == i)
+                k = EARLY_STEPS + i
+                picks[k] = [jnp.where(hit, at_f, picks[k][0]), jnp.where(hit, 1, picks[k][1])]
+            seen_e = seen_e + is_e.astype(jnp.int32)
+            seen_f = seen_f + is_f.astype(jnp.int32)
+        for k, (at, on) in enumerate(picks):
+            plan[g, 2 * k] = at
+            plan[g, 2 * k + 1] = on
+        return carry
+
+    def self_pairs(i, carry):
+        for k in range(4):
+            g = 4 * i + k
+            acc[g] = pair_sum(early_t[g], early_t[g], early_q[g])
+        return carry
+
+    def masked(g, k, t_ref, q_ref):
+        at = plan[g, 2 * k]
+        on = jnp.where(plan[g, 2 * k + 1] == 1, 1.0, 0.0)
+        return pair_sum(early_t[g], t_ref[at], q_ref[at]) * on
+
+    def early_pairs(i, carry):
+        for g in (2 * i, 2 * i + 1):
+            acc[g] += sum(masked(g, k, early_t, early_q) for k in range(EARLY_STEPS))
+        return carry
+
+    def fwd_pairs(i, carry):
+        for h in range(4):
+            g = 4 * i + h
+            acc[g] += sum(masked(g, EARLY_STEPS + k, fwd_t, fwd_q) for k in range(FWD_STEPS))
+        return carry
 
     def begin(i, state):
         axis, d, n = rounds[i]
@@ -307,6 +402,10 @@
     from_plus = (y == 2, y == 3)
 
     copies = begin(0, state)
+    for j in range(2):
+        for way in range(2):
+            late(1, way, j).start()
+    lax.fori_loop(0, BLK, plan_block, 0)
     for kind in (1, 0):
         for way in range(2):
             early(kind, way).wait_recv()
@@ -314,61 +413,96 @@
     def send_on(j, carry):
         for way in range(2):
             for kind in (1, 0):
-                fwd_copy(kind, way, j).start()
+                forward(kind, way, j).start()
         return carry
 
     lax.fori_loop(0, HALF, send_on, 0)
-    start_edges((1, 0), 0, HALF, *from_minus)
-    start_edges((1, 0), HALF, BLK, *from_plus)
-    for p in range(2):
+    start_edges((1, 0), (0, HALF), *from_minus, "early")
+    start_edges((1, 0), (HALF, BLK), *from_plus, "early")
+    for j in range(HALF):
         for way in range(2):
             for kind in (1, 0):
-                late(kind, way, p).start()
+                if not (kind == 1 and j < 2):
+                    late(kind, way, j).start()
+    keep = []
+    for kind in range(2):
+        for k, (at, size, there) in enumerate(
+            (
+                (0, BLK, mine),
+                (BLK, HALF, BLK + y_minus * BLK),
+                (BLK + HALF, HALF, BLK + y_plus * BLK + HALF),
+            )
+        ):
+            keep.append(
+                pltpu.make_async_copy(
+                    earlies[kind].at[pl.ds(at, size)], wins[kind].at[pl.ds(there, size)], keep_sem.at[kind, k]
+                )
+            )
+    for copy in keep:
+        copy.start()
     state = finish(0, copies)
 
     def far(j, carry):
         for way in range(2):
             for kind in (1, 0):
-                fwd_copy(kind, way, j).wait_recv()
+                forward(kind, way, j).wait_recv()
         for side, cond in ((0, y == 1), (1, y == 2)):
 
             @pl.when(cond & has[side])
             def _(side=side):
                 for way in range(2):
                     for kind in (1, 0):
-                        edge_copy(kind, side, way * HALF + j).start()
-
-        return carry
-
+                        edge_copy(kind, side, way * HALF + j, "far").start()
+
+        return carry
+
+    last = len(rounds) - 1
+    fill = {1: (0, 1), last - 1: (3, 4)} if last > 2 else {}
+    if last > 2:
+        fill[2] = (1, 3)
+    else:
+        fill = {1: (0, 4)}
     for i in range(1, len(rounds)):
         copies = begin(i, state)
-        if i == len(rounds) - 2:
+        if i == 1:
+            lax.fori_loop(0, 2, self_pairs, 0)
+        if i in fill:
+            lax.fori_loop(*fill[i], early_pairs, 0)
+        if i == last - 1:
             lax.fori_loop(0, HALF // 2, far, 0)
-        if i == len(rounds) - 1:
+        if i == last:
             lax.fori_loop(HALF // 2, HALF, far, 0)
         state = finish(i, copies)
+    for kind in range(2):
+        copy = pltpu.make_async_copy(fwds[kind], wins[kind].at[pl.ds(BLK + y_far * BLK, BLK)], keep_sem.at[kind, 3])
+        copy.start()
+        keep.append(copy)
     final[...] = state[1]
-    last = final[pl.ds(rank // 2 if leaf_count == 64 else 0, 1), :]
-    last = jnp.broadcast_to(last, (8, LANES))
-    root_ref[...] = jnp.where(lax.rem(rank, 2) == 1, pltpu.roll(last, DIM, 1), last)
-
-    for p in range(2):
+    line = final[pl.ds(rank // 2 if leaf_count == 64 else 0, 1), :]
+    line = jnp.broadcast_to(line, (8, LANES))
+    root_ref[...] = jnp.where(lax.rem(rank, 2) == 1, pltpu.roll(line, DIM, 1), line)
+
+    def second(j, carry):
         for way in range(2):
             for kind in (1, 0):
-                late(kind, way, p).wait_recv()
-        start_edges((1, 0), HALF + 2 * p, HALF + 2 * p + 2, *from_minus)
-        start_edges((1, 0), 2 * p, 2 * p + 2, *from_plus)
+                late(kind, way, j).wait_recv()
+        start_edges((1, 0), (HALF + j, HALF + j + 1), *from_minus, "late")
+        start_edges((1, 0), (j, j + 1), *from_plus, "late")
+        return carry
+
+    lax.fori_loop(0, 2, second, 0)
+    lax.fori_loop(0, 2, fwd_pairs, 0)
+    lax.fori_loop(2, HALF, second, 0)
 
     for kind in range(2):
         for way in range(2):
             early(kind, way).wait_send()
-            for p in range(2):
-                late(kind, way, p).wait_send()
 
     def drain(j, carry):
         for kind in range(2):
             for way in range(2):
-                fwd_copy(kind, way, j).wait_send()
+                forward(kind, way, j).wait_send()
+                late(kind, way, j).wait_send()
         return carry
 
     lax.fori_loop(0, HALF, drain, 0)
@@ -378,7 +512,7 @@
         def _(side=side):
             def body(j, carry):
                 for kind in range(2):
-                    edge_copy(kind, side, j).wait_send()
+                    edge_copy(kind, side, j, "late").wait_send()
                 return carry
 
             lax.fori_loop(0, BLK, body, 0)
@@ -387,42 +521,48 @@
         def _(side=side):
             def body(j, carry):
                 for kind in range(2):
-                    edge_copy(kind, side, j).wait_recv()
+                    edge_copy(kind, side, j, "late").wait_recv()
                 return carry
 
             lax.fori_loop(0, BLK, body, 0)
 
-
-def near_kernel(lists_ref, counts_ref, win_t, win_q, out_ref, flat_g, flat_c, acc, outs, sem_o):
-    start = lax.axis_index("leaf") * 32 - BLK
-    mine = BLK + lax.axis_index("sub") * BLK
+    for copy in keep:
+        copy.wait()
+
+
+def near_kernel(lists, counts, win_t, win_q, part_ref, out_ref, flat_g, flat_c, acc, outs, sem_o):
+    leaf = lax.axis_index("leaf")
+    y = lax.axis_index("sub")
+    mine = BLK + y * BLK
 
     def flatten(g, total):
         def one(s, carry):
-            flat_g[total + s] = g
-            flat_c[total + s] = lists_ref[g, s] - start
-            return carry
-
-        count = counts_ref[g]
-        lax.fori_loop(0, count, one, 0)
-        return total + count
-
-    total = lax.fori_loop(0, BLK, flatten, 0)
+            total, seen_e, seen_f = carry
+            block = lists[g, s]
+            is_e, _, is_f, _ = classify(block, leaf * 4 * BLK, y)
+            done = (is_e & (seen_e < EARLY_STEPS)) | (is_f & (seen_f < FWD_STEPS))
+            flat_g[total] = g
+            flat_c[total] = block - (leaf * 4 * BLK - BLK)
+            return (
+                total + jnp.where(done, 0, 1),
+                seen_e + is_e.astype(jnp.int32),
+                seen_f + is_f.astype(jnp.int32),
+            )
+
+        return lax.fori_loop(1, counts[g], one, (total, jnp.int32(0), jnp.int32(0)))[0]
+
+    total = lax.fori_loop(0, BLK, flatten, jnp.int32(0))
     for i in range(PAIRS - 1):
         flat_g[total + i] = BLK
         flat_c[total + i] = mine
-    acc[...] = jnp.zeros_like(acc)
+    acc[:BLK] = part_ref[...]
+    acc[BLK] = jnp.zeros((LEAF, LANES), F32)
 
     def step(i, carry):
         for k in range(PAIRS):
             g = flat_g[i * PAIRS + k]
             c = flat_c[i * PAIRS + k]
-            target = win_t[mine + jnp.minimum(g, BLK - 1)]
-            source = win_t[c]
-            left = jnp.concatenate([target, tail_rows(half_squares(target.astype(F32)), 0, 3)], axis=0)
-            right = jnp.concatenate([source, tail_rows(half_squares(source.astype(F32)), 3, 0)], axis=0)
-            weights = jnp.exp2(dot_tn(left, right) * SCALE).astype(BF16)
-            acc[g] += dot(weights, win_q[c])
+            acc[g] += pair_sum(win_t[mine + jnp.minimum(g, BLK - 1)], win_t[c], win_q[c])
         return carry
 
     lax.fori_loop(0, (total + PAIRS - 1) // PAIRS, step, 0)
@@ -446,15 +586,16 @@
     rounds = rounds_of(leaf_count)
     row_count = 7 + sum(n - 1 for _, _, n in rounds)
     dma = pltpu.SemaphoreType.DMA
-    win_t, win_q, root = pl.pallas_call(
+    win_t, win_q, part, root = pl.pallas_call(
         functools.partial(gather_kernel, leaf_count),
         out_shape=(
             jax.ShapeDtypeStruct((window, DIM, LEAF), BF16),
             jax.ShapeDtypeStruct((window, LEAF, LANES), BF16),
+            jax.ShapeDtypeStruct((BLK, LEAF, LANES), F32),
             jax.ShapeDtypeStruct((8, LANES), F32),
         ),
-        in_specs=[hbm] * 5,
-        out_specs=(vmem, vmem, vmem),
+        in_specs=[smem, smem] + [hbm] * 5,
+        out_specs=(vmem,) * 4,
         scratch_shapes=[
             pltpu.VMEM((DIM, BLK * LEAF), BF16),
             pltpu.VMEM((BLK * LEAF // LANES, LANES), jnp.int32),
@@ -464,12 +605,18 @@
             pltpu.VMEM((BLK, NODE, LANES), BF16),
             pltpu.VMEM((len(rounds), 4, NODE, LANES), BF16),
             pltpu.VMEM((SKEL, LANES), F32),
+            pltpu.VMEM((2 * BLK, DIM, LEAF), BF16),
+            pltpu.VMEM((2 * BLK, LEAF, LANES), BF16),
+            pltpu.VMEM((BLK, DIM, LEAF), BF16),
+            pltpu.VMEM((BLK, LEAF, LANES), BF16),
+            pltpu.SMEM((BLK, 2 * (EARLY_STEPS + FWD_STEPS)), jnp.int32),
             dma((4,)),
             dma((row_count,)),
+            dma((2, 4)),
             dma((2, 2)),
             dma((2, 2)),
-            dma((2, 2, 2)),
-            dma((2, 2, 2)),
+            dma((2, 2, HALF)),
+            dma((2, 2, HALF)),
             dma((2, 2, HALF)),
             dma((2, 2, HALF)),
             dma((2, 2, BLK)),
@@ -481,11 +628,11 @@
             collective_id=0, has_side_effects=True, vmem_limit_bytes=32 * 2**20
         ),
         name="gather_and_tree",
-    )(*map(in_hbm, (points.T, probes.reshape(BLK, LEAF, LANES), order.reshape(-1, LANES), leaf_sets, merge_sets)))
+    )(*map(in_hbm, (near_lists, near_counts, points.T, probes.reshape(BLK, LEAF, LANES), order.reshape(-1, LANES), leaf_sets, merge_sets)))
     near = pl.pallas_call(
         near_kernel,
         out_shape=jax.ShapeDtypeStruct((BLK, LEAF, LANES), F32),
-        in_specs=[smem, smem, vmem, vmem],
+        in_specs=[smem, smem, vmem, vmem, vmem],
         out_specs=hbm,
         scratch_shapes=[
             pltpu.SMEM((128,), jnp.int32),
@@ -496,7 +643,7 @@
         ],
         compiler_params=pltpu.CompilerParams(vmem_limit_bytes=32 * 2**20),
         name="near_field",
-    )(in_hbm(near_lists), in_hbm(near_counts), win_t, win_q)
+    )(in_hbm(near_lists), in_hbm(near_counts), win_t, win_q, part)
     return near.reshape(BLK * LEAF, LANES), root[0, :DIM]
 
 

time: 94.2 us -> 88.3 us (0.937)
  the two profiles are of different devices: /device:TPU:48 before, /device:TPU:72 now
where the time goes in v4:
time: 88.3 us; the launch traced here: 88.2 us
  Pallas kernels  87 us (99%)
    pallas_call x1, Pallas kernels, on_device(): pl.pallas_call(functools.partial(gather_kernel, leaf_count), out_shape=(j...  77.5 us
    pallas_call x1, Pallas kernels, on_device(): pl.pallas_call(near_kernel, out_shape=jax.ShapeDtypeStruct((BLK, LEAF, LA...  9.57 us

profile of v4, /device:TPU:72, one launch (start us, length us, event | category | flops | bytes accessed | tf_op | source)
XLA Modules:
  0.0 88.2 jit_solution(6267501715141457424)
XLA Ops:
  0.6 77.5 %gather_and_tree.1 = (bf16[48,64,512]{2,1,0:T(8,128)(2,1)S(1)}, bf16[48,512,128]{2,1,0:T(8,128)(2,1)S(1)}, f32[8,512,128]{2,1,0:T(8,128)S(1)}, f32[8,128]{1,0:T(8,128)S(1)}) custom-call(s32[8,12]{1,0:T(8,128)} %lists.3, s32[8]{0:T(128)} %counts.3, bf16[64,4096]{1,0:T(8,128)(2,1)} %bitcast.8, bf16[8,512,128]{2,1,0:T(8,128)(2,1)} %bitcast.7, ...), custom_call_target="tpu_custom_call" | custom-call | tf_op jit(solution)/shard_map/gather_and_tree/pallas_call | solution.py:589
  78.1 9.6 %near_field.1 = f32[8,512,128]{2,1,0:T(8,128)} custom-call(s32[8,12]{1,0:T(8,128)} %lists.3, s32[8]{0:T(128)} %counts.3, bf16[48,64,512]{2,1,0:T(8,128)(2,1)S(1)} %get-tuple-element.6.win_t, bf16[48,512,128]{2,1,0:T(8,128)(2,1)S(1)} %get-tuple-element.7.win_q, f32[8,512,128]{2,1,0:T(8,128)S(1)} %get-tuple-element.8.part_ref), custom_call_target="tpu_custom_call" | custom-call | tf_op jit(solution)/shard_map/near_field/pallas_call | solution.py:632
  87.7 0.5 slice_bitcast_fusion

commit v5 on v4

--- a/solution.py
+++ b/solution.py
@@ -19,8 +19,7 @@
 SKEL = 128
 NODE = FORM + 2 * SKEL
 PAIRS = 4
-EARLY_STEPS = 2
-FWD_STEPS = 1
+STEPS = (2, 1, 1)
 LOG2E = 1.4426950408889634
 SCALE = 2.0 * LOG2E / DIM
 
@@ -110,7 +109,10 @@
     j = at & (BLK - 1)
     off = (lax.shift_right_arithmetic(at, 3) - y) & 3
     early = inside & ((off == 0) | ((off == 3) & (j < HALF)) | ((off == 1) & (j >= HALF)))
-    return early, j + jnp.where(off == 0, 0, BLK), inside & (off == 2), j
+    side = jnp.where(at < 0, 0, 1)
+    last = (side == (y & 1)) & ((j < HALF) == (y >= 2))
+    edge = jnp.logical_not(inside) & jnp.logical_not(last)
+    return [(early, j + jnp.where(off == 0, 0, BLK)), (inside & (off == 2), j), (edge, side * BLK + j)]
 
 
 def gather_kernel(
@@ -138,6 +140,8 @@
     early_q,
     fwd_t,
     fwd_q,
+    edge_t,
+    edge_q,
     plan,
     in_sem,
     row_sem,
@@ -205,6 +209,9 @@
     wins = (win_t, win_q)
     earlies = (early_t, early_q)
     fwds = (fwd_t, fwd_q)
+    edges = (edge_t, edge_q)
+    near_side = y & 1
+    soon = (y // 2) * HALF
 
     def remote(src, dst, send, recv, who):
         return pltpu.make_async_remote_copy(
@@ -252,9 +259,10 @@
             src = fwds[kind].at[pl.ds(j, 1)]
         else:
             src = wins[kind].at[pl.ds(BLK + (3 * BLK if side == 0 else 0) + j, 1)]
+        there = wins[kind].at[pl.ds((0 if side == 0 else 5 * BLK) + j, 1)]
         return remote(
             src,
-            wins[kind].at[pl.ds((0 if side == 0 else 5 * BLK) + j, 1)],
+            there if source == "late" else edges[kind].at[pl.ds(side * BLK + j, 1)],
             edge_send.at[kind, side, j],
             edge_recv.at[kind, side, j],
             up if side == 0 else down,
@@ -330,27 +338,25 @@
     merge_all(2, 1, 4)
     state = merge(nodes[0], nodes[1], row(3))
 
+    stocks = ((early_t, early_q), (fwd_t, fwd_q), (edge_t, edge_q))
+    spare = (0, 0, jnp.where(leaf > 0, 0, BLK) + soon)
+    first_step = (0, STEPS[0], STEPS[0] + STEPS[1])
+
     def plan_block(g, carry):
         count = counts[g]
-        picks = [[g, 0] for _ in range(EARLY_STEPS)] + [[0, 0] for _ in range(FWD_STEPS)]
-        seen_e = 0
-        seen_f = 0
+        picks = [[[spare[c], 0] for _ in range(STEPS[c])] for c in range(3)]
+        seen = [0, 0, 0]
         for s in range(1, lists.shape[1]):
-            is_e, at_e, is_f, at_f = classify(lists[g, s], leaf * 4 * BLK, y)
-            is_e = is_e & (s < count)
-            is_f = is_f & (s < count)
-            for i in range(EARLY_STEPS):
-                hit = is_e & (seen_e == i)
-                picks[i] = [jnp.where(hit, at_e, picks[i][0]), jnp.where(hit, 1, picks[i][1])]
-            for i in range(FWD_STEPS):
-                hit = is_f & (seen_f == i)
-                k = EARLY_STEPS + i
-                picks[k] = [jnp.where(hit, at_f, picks[k][0]), jnp.where(hit, 1, picks[k][1])]
-            seen_e = seen_e + is_e.astype(jnp.int32)
-            seen_f = seen_f + is_f.astype(jnp.int32)
-        for k, (at, on) in enumerate(picks):
-            plan[g, 2 * k] = at
-            plan[g, 2 * k + 1] = on
+            for c, (there, at) in enumerate(classify(lists[g, s], leaf * 4 * BLK, y)):
+                there = there & (s < count)
+                for pick, i in zip(picks[c], range(STEPS[c])):
+                    hit = there & (seen[c] == i)
+                    pick[:] = jnp.where(hit, at, pick[0]), jnp.where(hit, 1, pick[1])
+                seen[c] = seen[c] + there.astype(jnp.int32)
+        for c in range(3):
+            for i in range(STEPS[c]):
+                plan[g, 2 * (first_step[c] + i)] = picks[c][i][0]
+                plan[g, 2 * (first_step[c] + i) + 1] = picks[c][i][1]
         return carry
 
     def self_pairs(i, carry):
@@ -359,21 +365,21 @@
             acc[g] = pair_sum(early_t[g], early_t[g], early_q[g])
         return carry
 
-    def masked(g, k, t_ref, q_ref):
-        at = plan[g, 2 * k]
-        on = jnp.where(plan[g, 2 * k + 1] == 1, 1.0, 0.0)
-        return pair_sum(early_t[g], t_ref[at], q_ref[at]) * on
-
-    def early_pairs(i, carry):
-        for g in (2 * i, 2 * i + 1):
-            acc[g] += sum(masked(g, k, early_t, early_q) for k in range(EARLY_STEPS))
-        return carry
-
-    def fwd_pairs(i, carry):
-        for h in range(4):
-            g = 4 * i + h
-            acc[g] += sum(masked(g, EARLY_STEPS + k, fwd_t, fwd_q) for k in range(FWD_STEPS))
-        return carry
+    def pairs_from(c):
+        width = 4 // STEPS[c]
+
+        def body(i, carry):
+            for h in range(width):
+                g = width * i + h
+                total = acc[g]
+                for k in range(first_step[c], first_step[c] + STEPS[c]):
+                    at = plan[g, 2 * k]
+                    on = jnp.where(plan[g, 2 * k + 1] == 1, 1.0, 0.0)
+                    total = total + pair_sum(early_t[g], stocks[c][0][at], stocks[c][1][at]) * on
+                acc[g] = total
+            return carry
+
+        return body
 
     def begin(i, state):
         axis, d, n = rounds[i]
@@ -402,10 +408,10 @@
     from_plus = (y == 2, y == 3)
 
     copies = begin(0, state)
-    for j in range(2):
-        for way in range(2):
-            late(1, way, j).start()
+    for way in range(2):
+        late(1, way, 0).start()
     lax.fori_loop(0, BLK, plan_block, 0)
+    lax.fori_loop(0, 2, self_pairs, 0)
     for kind in (1, 0):
         for way in range(2):
             early(kind, way).wait_recv()
@@ -422,7 +428,7 @@
     for j in range(HALF):
         for way in range(2):
             for kind in (1, 0):
-                if not (kind == 1 and j < 2):
+                if not (kind == 1 and j == 0):
                     late(kind, way, j).start()
     keep = []
     for kind in range(2):
@@ -457,21 +463,19 @@
         return carry
 
     last = len(rounds) - 1
-    fill = {1: (0, 1), last - 1: (3, 4)} if last > 2 else {}
-    if last > 2:
-        fill[2] = (1, 3)
+    e_step, f_step = pairs_from(0), pairs_from(1)
+    if last == 4:
+        fill = {
+            2: ((e_step, 0, 1), (far, 0, 1), (e_step, 1, 2), (far, 1, 2)),
+            3: ((e_step, 2, 3), (far, 2, 3), (e_step, 3, 4), (far, 3, 4)),
+            4: ((f_step, 0, 2),),
+        }
     else:
-        fill = {1: (0, 4)}
+        fill = {last: ((e_step, 0, 4), (far, 0, 4), (f_step, 0, 2))}
     for i in range(1, len(rounds)):
         copies = begin(i, state)
-        if i == 1:
-            lax.fori_loop(0, 2, self_pairs, 0)
-        if i in fill:
-            lax.fori_loop(*fill[i], early_pairs, 0)
-        if i == last - 1:
-            lax.fori_loop(0, HALF // 2, far, 0)
-        if i == last:
-            lax.fori_loop(HALF // 2, HALF, far, 0)
+        for what, start, end in fill.get(i, ()):
+            lax.fori_loop(start, end, what, 0)
         state = finish(i, copies)
     for kind in range(2):
         copy = pltpu.make_async_copy(fwds[kind], wins[kind].at[pl.ds(BLK + y_far * BLK, BLK)], keep_sem.at[kind, 3])
@@ -490,9 +494,41 @@
         start_edges((1, 0), (j, j + 1), *from_plus, "late")
         return carry
 
-    lax.fori_loop(0, 2, second, 0)
-    lax.fori_loop(0, 2, fwd_pairs, 0)
-    lax.fori_loop(2, HALF, second, 0)
+    def await_edges(near_from, others):
+        for side in range(2):
+
+            @pl.when(has[1 - side])
+            def _(side=side):
+                def body(j, carry):
+                    for kind in range(2):
+                        edge_copy(kind, side, j, "late" if not others else "far").wait_recv()
+                    return carry
+
+                @pl.when(near_side == side)
+                def _():
+                    lax.fori_loop(near_from, near_from + HALF, body, 0)
+
+                if others:
+
+                    @pl.when(near_side != side)
+                    def _():
+                        lax.fori_loop(0, BLK, body, 0)
+
+    lax.fori_loop(0, HALF, second, 0)
+    await_edges(soon, True)
+    for kind in range(2):
+        for k, (at, size, there) in enumerate(
+            (
+                (near_side * BLK + soon, HALF, near_side * 5 * BLK + soon),
+                ((1 - near_side) * BLK, BLK, (1 - near_side) * 5 * BLK),
+            )
+        ):
+            copy = pltpu.make_async_copy(
+                edges[kind].at[pl.ds(at, size)], wins[kind].at[pl.ds(there, size)], keep_sem.at[kind, 4 + k]
+            )
+            copy.start()
+            keep.append(copy)
+    lax.fori_loop(0, BLK * STEPS[2] // 4, pairs_from(2), 0)
 
     for kind in range(2):
         for way in range(2):
@@ -517,15 +553,7 @@
 
             lax.fori_loop(0, BLK, body, 0)
 
-        @pl.when(has[1 - side])
-        def _(side=side):
-            def body(j, carry):
-                for kind in range(2):
-                    edge_copy(kind, side, j, "late").wait_recv()
-                return carry
-
-            lax.fori_loop(0, BLK, body, 0)
-
+    await_edges(HALF - soon, False)
     for copy in keep:
         copy.wait()
 
@@ -537,19 +565,18 @@
 
     def flatten(g, total):
         def one(s, carry):
-            total, seen_e, seen_f = carry
+            total, *seen = carry
             block = lists[g, s]
-            is_e, _, is_f, _ = classify(block, leaf * 4 * BLK, y)
-            done = (is_e & (seen_e < EARLY_STEPS)) | (is_f & (seen_f < FWD_STEPS))
+            done = False
+            for c, (there, _) in enumerate(classify(block, leaf * 4 * BLK, y)):
+                done = done | (there & (seen[c] < STEPS[c]))
+                seen[c] = seen[c] + there.astype(jnp.int32)
             flat_g[total] = g
             flat_c[total] = block - (leaf * 4 * BLK - BLK)
-            return (
-                total + jnp.where(done, 0, 1),
-                seen_e + is_e.astype(jnp.int32),
-                seen_f + is_f.astype(jnp.int32),
-            )
-
-        return lax.fori_loop(1, counts[g], one, (total, jnp.int32(0), jnp.int32(0)))[0]
+            return (total + jnp.where(done, 0, 1), *seen)
+
+        zero = jnp.int32(0)
+        return lax.fori_loop(1, counts[g], one, (total, zero, zero, zero))[0]
 
     total = lax.fori_loop(0, BLK, flatten, jnp.int32(0))
     for i in range(PAIRS - 1):
@@ -609,10 +636,12 @@
             pltpu.VMEM((2 * BLK, LEAF, LANES), BF16),
             pltpu.VMEM((BLK, DIM, LEAF), BF16),
             pltpu.VMEM((BLK, LEAF, LANES), BF16),
-            pltpu.SMEM((BLK, 2 * (EARLY_STEPS + FWD_STEPS)), jnp.int32),
+            pltpu.VMEM((2 * BLK, DIM, LEAF), BF16),
+            pltpu.VMEM((2 * BLK, LEAF, LANES), BF16),
+            pltpu.SMEM((BLK, 2 * sum(STEPS)), jnp.int32),
             dma((4,)),
             dma((row_count,)),
-            dma((2, 4)),
+            dma((2, 6)),
             dma((2, 2)),
             dma((2, 2)),
             dma((2, 2, HALF)),

time: 88.3 us -> 86.9 us (0.984)
  the two profiles are of different devices: /device:TPU:72 before, /device:TPU:109 now
where the time goes in v5:
time: 86.9 us; the launch traced here: 87.7 us
  Pallas kernels  86.5 us (100%)
    pallas_call x1, Pallas kernels, on_device(): pl.pallas_call(functools.partial(gather_kernel, leaf_count), out_shape=(j...  75.1 us
    pallas_call x1, Pallas kernels, on_device(): pl.pallas_call(near_kernel, out_shape=jax.ShapeDtypeStruct((BLK, LEAF, LA...  11.4 us

profile of v5, /device:TPU:109, one launch (start us, length us, event | category | flops | bytes accessed | tf_op | source)
XLA Modules:
  0.0 87.7 jit_solution(10839965567719923997)
XLA Ops:
  0.6 75.1 %gather_and_tree.1 = (bf16[48,64,512]{2,1,0:T(8,128)(2,1)S(1)}, bf16[48,512,128]{2,1,0:T(8,128)(2,1)S(1)}, f32[8,512,128]{2,1,0:T(8,128)S(1)}, f32[8,128]{1,0:T(8,128)S(1)}) custom-call(s32[8,12]{1,0:T(8,128)} %lists.3, s32[8]{0:T(128)} %counts.3, bf16[64,4096]{1,0:T(8,128)(2,1)} %bitcast.8, bf16[8,512,128]{2,1,0:T(8,128)(2,1)} %bitcast.7, ...), custom_call_target="tpu_custom_call" | custom-call | tf_op jit(solution)/shard_map/gather_and_tree/pallas_call | solution.py:616
  75.8 11.4 %near_field.1 = f32[8,512,128]{2,1,0:T(8,128)} custom-call(s32[8,12]{1,0:T(8,128)} %lists.3, s32[8]{0:T(128)} %counts.3, bf16[48,64,512]{2,1,0:T(8,128)(2,1)S(1)} %get-tuple-element.6.win_t, bf16[48,512,128]{2,1,0:T(8,128)(2,1)S(1)} %get-tuple-element.7.win_q, f32[8,512,128]{2,1,0:T(8,128)S(1)} %get-tuple-element.8.part_ref), custom_call_target="tpu_custom_call" | custom-call | tf_op jit(solution)/shard_map/near_field/pallas_call | solution.py:661
  87.2 0.5 slice_bitcast_fusion

commit v6 on v5

--- a/solution.py
+++ b/solution.py
@@ -19,7 +19,7 @@
 SKEL = 128
 NODE = FORM + 2 * SKEL
 PAIRS = 4
-STEPS = (2, 1, 1)
+STEPS = (2, 2, 2, 1)
 LOG2E = 1.4426950408889634
 SCALE = 2.0 * LOG2E / DIM
 
@@ -108,11 +108,11 @@
     inside = (at >= 0) & (at < 4 * BLK)
     j = at & (BLK - 1)
     off = (lax.shift_right_arithmetic(at, 3) - y) & 3
-    early = inside & ((off == 0) | ((off == 3) & (j < HALF)) | ((off == 1) & (j >= HALF)))
+    early = inside & (((off == 3) & (j < HALF)) | ((off == 1) & (j >= HALF)))
     side = jnp.where(at < 0, 0, 1)
     last = (side == (y & 1)) & ((j < HALF) == (y >= 2))
     edge = jnp.logical_not(inside) & jnp.logical_not(last)
-    return [(early, j + jnp.where(off == 0, 0, BLK)), (inside & (off == 2), j), (edge, side * BLK + j)]
+    return [(inside & (off == 0), j), (early, j), (inside & (off == 2), j), (edge, side * BLK + j)]
 
 
 def gather_kernel(
@@ -136,6 +136,8 @@
     nodes,
     tree,
     final,
+    own_t,
+    own_q,
     early_t,
     early_q,
     fwd_t,
@@ -181,7 +183,7 @@
         pltpu.make_async_copy(order_hbm, order, in_sem.at[0]),
         pltpu.make_async_copy(points_hbm, points, in_sem.at[1]),
         pltpu.make_async_copy(sets_hbm, sets, in_sem.at[2]),
-        pltpu.make_async_copy(probes_hbm, early_q.at[pl.ds(0, BLK)], in_sem.at[3]),
+        pltpu.make_async_copy(probes_hbm, own_q, in_sem.at[3]),
     ]
     wanted = [first_block + i for i in range(7)]
     row_at = []
@@ -207,6 +209,7 @@
     pl.semaphore_wait(barrier, len(greet))
 
     wins = (win_t, win_q)
+    owns = (own_t, own_q)
     earlies = (early_t, early_q)
     fwds = (fwd_t, fwd_q)
     edges = (edge_t, edge_q)
@@ -219,12 +222,12 @@
         )
 
     def own(kind, at, size):
-        return (probes_hbm if kind else early_t).at[pl.ds(at, size)]
+        return (probes_hbm if kind else own_t).at[pl.ds(at, size)]
 
     def early(kind, way):
         return remote(
             own(kind, way * HALF, HALF),
-            earlies[kind].at[pl.ds(BLK + way * HALF, HALF)],
+            earlies[kind].at[pl.ds(way * HALF, HALF)],
             own_send.at[kind, way],
             own_recv.at[kind, way],
             minus if way else plus,
@@ -243,7 +246,7 @@
     def forward(kind, way, j):
         at = way * HALF + j
         return remote(
-            earlies[kind].at[pl.ds(BLK + at, 1)],
+            earlies[kind].at[pl.ds(at, 1)],
             fwds[kind].at[pl.ds(at, 1)],
             fwd_send.at[kind, way, j],
             fwd_recv.at[kind, way, j],
@@ -254,7 +257,7 @@
         if source == "own":
             src = own(kind, j, 1)
         elif source == "early":
-            src = earlies[kind].at[pl.ds(BLK + j, 1)]
+            src = earlies[kind].at[pl.ds(j, 1)]
         elif source == "far":
             src = fwds[kind].at[pl.ds(j, 1)]
         else:
@@ -295,7 +298,7 @@
             to = jnp.concatenate([order[pl.ds(b * 4 + q, 1), :] for q in range(4)], axis=1)
             at = pl.ds(pl.multiple_of(b * LEAF, LEAF), LEAF)
             coords = dot(points[:, at], one_hot(to, LEAF))
-            early_t[b] = coords.astype(BF16)
+            own_t[b] = coords.astype(BF16)
             own_h[b] = tail_rows(half_squares(coords), 0, None)
         return carry
 
@@ -310,8 +313,8 @@
     def leaf_nodes(i, carry):
         for k in range(4):
             b = 4 * i + k
-            coords = jnp.concatenate([early_t[b], own_h[b]], axis=0)
-            probe = early_q[b]
+            coords = jnp.concatenate([own_t[b], own_h[b]], axis=0)
+            probe = own_q[b]
             hot = one_hot(sets[pl.ds(b, 1), :], LEAF)
             picked = dot(coords, hot)
             kept = dot_tn(hot, probe)
@@ -338,14 +341,14 @@
     merge_all(2, 1, 4)
     state = merge(nodes[0], nodes[1], row(3))
 
-    stocks = ((early_t, early_q), (fwd_t, fwd_q), (edge_t, edge_q))
-    spare = (0, 0, jnp.where(leaf > 0, 0, BLK) + soon)
-    first_step = (0, STEPS[0], STEPS[0] + STEPS[1])
+    stocks = ((own_t, own_q), (early_t, early_q), (fwd_t, fwd_q), (edge_t, edge_q))
+    spare = (0, 0, 0, jnp.where(leaf > 0, 0, BLK) + soon)
+    first_step = [sum(STEPS[:c]) for c in range(4)]
 
     def plan_block(g, carry):
         count = counts[g]
-        picks = [[[spare[c], 0] for _ in range(STEPS[c])] for c in range(3)]
-        seen = [0, 0, 0]
+        picks = [[[spare[c], 0] for _ in range(STEPS[c])] for c in range(4)]
+        seen = [0, 0, 0, 0]
         for s in range(1, lists.shape[1]):
             for c, (there, at) in enumerate(classify(lists[g, s], leaf * 4 * BLK, y)):
                 there = there & (s < count)
@@ -353,7 +356,7 @@
                     hit = there & (seen[c] == i)
                     pick[:] = jnp.where(hit, at, pick[0]), jnp.where(hit, 1, pick[1])
                 seen[c] = seen[c] + there.astype(jnp.int32)
-        for c in range(3):
+        for c in range(4):
             for i in range(STEPS[c]):
                 plan[g, 2 * (first_step[c] + i)] = picks[c][i][0]
                 plan[g, 2 * (first_step[c] + i) + 1] = picks[c][i][1]
@@ -362,7 +365,7 @@
     def self_pairs(i, carry):
         for k in range(4):
             g = 4 * i + k
-            acc[g] = pair_sum(early_t[g], early_t[g], early_q[g])
+            acc[g] = pair_sum(own_t[g], own_t[g], own_q[g])
         return carry
 
     def pairs_from(c):
@@ -375,7 +378,7 @@
                 for k in range(first_step[c], first_step[c] + STEPS[c]):
                     at = plan[g, 2 * k]
                     on = jnp.where(plan[g, 2 * k + 1] == 1, 1.0, 0.0)
-                    total = total + pair_sum(early_t[g], stocks[c][0][at], stocks[c][1][at]) * on
+                    total = total + pair_sum(own_t[g], stocks[c][0][at], stocks[c][1][at]) * on
                 acc[g] = total
             return carry
 
@@ -412,6 +415,7 @@
         late(1, way, 0).start()
     lax.fori_loop(0, BLK, plan_block, 0)
     lax.fori_loop(0, 2, self_pairs, 0)
+    lax.fori_loop(0, 4, pairs_from(0), 0)
     for kind in (1, 0):
         for way in range(2):
             early(kind, way).wait_recv()
@@ -432,18 +436,15 @@
                     late(kind, way, j).start()
     keep = []
     for kind in range(2):
-        for k, (at, size, there) in enumerate(
+        for k, (ref, there) in enumerate(
             (
-                (0, BLK, mine),
-                (BLK, HALF, BLK + y_minus * BLK),
-                (BLK + HALF, HALF, BLK + y_plus * BLK + HALF),
+                (owns[kind], mine),
+                (earlies[kind].at[pl.ds(0, HALF)], BLK + y_minus * BLK),
+                (earlies[kind].at[pl.ds(HALF, HALF)], BLK + y_plus * BLK + HALF),
             )
         ):
-            keep.append(
-                pltpu.make_async_copy(
-                    earlies[kind].at[pl.ds(at, size)], wins[kind].at[pl.ds(there, size)], keep_sem.at[kind, k]
-                )
-            )
+            size = HALF if k else BLK
+            keep.append(pltpu.make_async_copy(ref, wins[kind].at[pl.ds(there, size)], keep_sem.at[kind, k]))
     for copy in keep:
         copy.start()
     state = finish(0, copies)
@@ -463,7 +464,7 @@
         return carry
 
     last = len(rounds) - 1
-    e_step, f_step = pairs_from(0), pairs_from(1)
+    e_step, f_step = pairs_from(1), pairs_from(2)
     if last == 4:
         fill = {
             2: ((e_step, 0, 1), (far, 0, 1), (e_step, 1, 2), (far, 1, 2)),
@@ -514,7 +515,9 @@
                     def _():
                         lax.fori_loop(0, BLK, body, 0)
 
-    lax.fori_loop(0, HALF, second, 0)
+    lax.fori_loop(0, 1, second, 0)
+    lax.fori_loop(2, 4, f_step, 0)
+    lax.fori_loop(1, HALF, second, 0)
     await_edges(soon, True)
     for kind in range(2):
         for k, (at, size, there) in enumerate(
@@ -528,7 +531,7 @@
             )
             copy.start()
             keep.append(copy)
-    lax.fori_loop(0, BLK * STEPS[2] // 4, pairs_from(2), 0)
+    lax.fori_loop(0, BLK * STEPS[3] // 4, pairs_from(3), 0)
 
     for kind in range(2):
         for way in range(2):
@@ -558,7 +561,7 @@
         copy.wait()
 
 
-def near_kernel(lists, counts, win_t, win_q, part_ref, out_ref, flat_g, flat_c, acc, outs, sem_o):
+def near_kernel(lists, counts, win_t, win_q, part_ref, root_ref, out_ref, root_out, flat_g, flat_c, ends, acc, outs, sem_o):
     leaf = lax.axis_index("leaf")
     y = lax.axis_index("sub")
     mine = BLK + y * BLK
@@ -575,8 +578,9 @@
             flat_c[total] = block - (leaf * 4 * BLK - BLK)
             return (total + jnp.where(done, 0, 1), *seen)
 
-        zero = jnp.int32(0)
-        return lax.fori_loop(1, counts[g], one, (total, zero, zero, zero))[0]
+        total = lax.fori_loop(1, counts[g], one, (total, *([jnp.int32(0)] * 4)))[0]
+        ends[g] = total
+        return total
 
     total = lax.fori_loop(0, BLK, flatten, jnp.int32(0))
     for i in range(PAIRS - 1):
@@ -592,10 +596,15 @@
             acc[g] += pair_sum(win_t[mine + jnp.minimum(g, BLK - 1)], win_t[c], win_q[c])
         return carry
 
-    lax.fori_loop(0, (total + PAIRS - 1) // PAIRS, step, 0)
-    for g in range(BLK):
+    def block(g, i):
+        until = jnp.maximum(i, (ends[g] + PAIRS - 1) // PAIRS)
+        lax.fori_loop(i, until, step, 0)
         outs[g] = acc[g] * (LEAF**-0.5)
         pltpu.make_async_copy(outs.at[g], out_ref.at[g], sem_o.at[g]).start()
+        return until
+
+    lax.fori_loop(0, BLK, block, jnp.int32(0))
+    root_out[...] = root_ref[0:1, :DIM]
     for g in range(BLK):
         pltpu.make_async_copy(outs.at[g], out_ref.at[g], sem_o.at[g]).wait()
 
@@ -632,8 +641,10 @@
             pltpu.VMEM((BLK, NODE, LANES), BF16),
             pltpu.VMEM((len(rounds), 4, NODE, LANES), BF16),
             pltpu.VMEM((SKEL, LANES), F32),
-            pltpu.VMEM((2 * BLK, DIM, LEAF), BF16),
-            pltpu.VMEM((2 * BLK, LEAF, LANES), BF16),
+            pltpu.VMEM((BLK, DIM, LEAF), BF16),
+            pltpu.VMEM((BLK, LEAF, LANES), BF16),
+            pltpu.VMEM((BLK, DIM, LEAF), BF16),
+            pltpu.VMEM((BLK, LEAF, LANES), BF16),
             pltpu.VMEM((BLK, DIM, LEAF), BF16),
             pltpu.VMEM((BLK, LEAF, LANES), BF16),
             pltpu.VMEM((2 * BLK, DIM, LEAF), BF16),
@@ -658,22 +669,23 @@
         ),
         name="gather_and_tree",
     )(*map(in_hbm, (near_lists, near_counts, points.T, probes.reshape(BLK, LEAF, LANES), order.reshape(-1, LANES), leaf_sets, merge_sets)))
-    near = pl.pallas_call(
+    near, root = pl.pallas_call(
         near_kernel,
-        out_shape=jax.ShapeDtypeStruct((BLK, LEAF, LANES), F32),
-        in_specs=[smem, smem, vmem, vmem, vmem],
-        out_specs=hbm,
+        out_shape=(jax.ShapeDtypeStruct((BLK, LEAF, LANES), F32), jax.ShapeDtypeStruct((1, DIM), F32)),
+        in_specs=[smem, smem, vmem, vmem, vmem, vmem],
+        out_specs=(hbm, vmem),
         scratch_shapes=[
             pltpu.SMEM((128,), jnp.int32),
             pltpu.SMEM((128,), jnp.int32),
+            pltpu.SMEM((BLK,), jnp.int32),
             pltpu.VMEM((BLK + 1, LEAF, LANES), F32),
             pltpu.VMEM((BLK, LEAF, LANES), F32),
             dma((BLK,)),
         ],
         compiler_params=pltpu.CompilerParams(vmem_limit_bytes=32 * 2**20),
         name="near_field",
-    )(in_hbm(near_lists), in_hbm(near_counts), win_t, win_q, part)
-    return near.reshape(BLK * LEAF, LANES), root[0, :DIM]
+    )(in_hbm(near_lists), in_hbm(near_counts), win_t, win_q, part, root)
+    return near.reshape(BLK * LEAF, LANES), root.reshape(DIM)
 
 
 def solution(mesh):

time: 86.9 us -> 88.6 us (1.020)
  the two profiles are of different devices: /device:TPU:109 before, /device:TPU:48 now
where the time goes in v6:
time: 88.6 us; the launch traced here: 88 us
  Pallas kernels  87.2 us (98%)
    pallas_call x1, Pallas kernels, on_device(): pl.pallas_call(functools.partial(gather_kernel, leaf_count), out_shape=(j...  76.7 us
    pallas_call x1, Pallas kernels, on_device(): pl.pallas_call(near_kernel, out_shape=(jax.ShapeDtypeStruct((BLK, LEAF, L...  10.5 us

profile of v6, /device:TPU:48, one launch (start us, length us, event | category | flops | bytes accessed | tf_op | source)
XLA Modules:
  0.0 88.0 jit_solution(16345267159852326395)
XLA Ops:
  0.6 76.7 %gather_and_tree.1 = (bf16[48,64,512]{2,1,0:T(8,128)(2,1)S(1)}, bf16[48,512,128]{2,1,0:T(8,128)(2,1)S(1)}, f32[8,512,128]{2,1,0:T(8,128)S(1)}, f32[8,128]{1,0:T(8,128)S(1)}) custom-call(s32[8,12]{1,0:T(8,128)} %lists.3, s32[8]{0:T(128)} %counts.3, bf16[64,4096]{1,0:T(8,128)(2,1)} %bitcast.6, bf16[8,512,128]{2,1,0:T(8,128)(2,1)} %bitcast.5, ...), custom_call_target="tpu_custom_call" | custom-call | tf_op jit(solution)/shard_map/gather_and_tree/pallas_call | solution.py:625
  77.3 10.5 %near_field.1 = (f32[8,512,128]{2,1,0:T(8,128)}, f32[1,64]{1,0:T(1,128)}) custom-call(s32[8,12]{1,0:T(8,128)} %lists.3, s32[8]{0:T(128)} %counts.3, bf16[48,64,512]{2,1,0:T(8,128)(2,1)S(1)} %get-tuple-element.8.win_t, bf16[48,512,128]{2,1,0:T(8,128)(2,1)S(1)} %get-tuple-element.9.win_q, f32[8,512,128]{2,1,0:T(8,128)S(1)} %get-tuple-element.10.part_ref, ...), custom_call_target="tpu_custom_call" | custom-call | tf_op jit(solution)/shard_map/near_field/pallas_call | solution.py:672
